TPU v7x, 32 devices: a whole 2x2x4 slice. The times are simulated.
32 devices in a mesh: lsec: 8 (over z, x), rsec: 4 (over y, core).
Axes of the slice: x: 2, y: 2, z: 4, core: 2. Of those that a mesh axis runs over, the one named last changes fastest.
Arguments:
- states: float32 [2, 5120, 2560], P(None, 'lsec', 'rsec'), may hold values from -6 to 6
- left_env: float32 [8, 640, 640], P('lsec', 'rsec'), may hold values from -0.25 to 0.25
- right_env: float32 [4, 640, 640], P('rsec', 'lsec'), may hold values from -0.25 to 0.25
- left_op: float32 [8, 640, 640], P('lsec', 'rsec'), may hold values from -0.25 to 0.25
- right_op: float32 [4, 640, 640], P('rsec', 'lsec'), may hold values from -0.25 to 0.25
- sizes_left: int32 [8], P('lsec'), may hold values from 320 to 640
- sizes_right: int32 [4], P('rsec'), may hold values from 320 to 640
Outputs:
- applied: float32 [2, 5120, 2560], P(None, 'lsec', 'rsec')
All inputs are finite; a program needn't handle non-finite values.
Results may differ from a plain program's by a relative error of at most 0.000059.
Values sent between devices are 32-bit elements; how exact they have to be, the bound alone decides.
No kernel may reach another device: no remote copies, remote signals or barrier semaphores. Data moves between devices by JAX's collectives and lax.ppermute only.
A program may use at most 128 MiB of HBM per device.

v0:
```python
import jax
import jax.numpy as jnp
from jax import lax
from jax.experimental import pallas as pl
from jax.experimental.pallas import tpu as pltpu
from jax.sharding import PartitionSpec as P

AXES = ("lsec", "rsec")
RETURNS = (2, 2, 1)
TWIN = (2, 3)
F32, BF16 = jnp.float32, jnp.bfloat16
MIB = 1024 * 1024


def split(x):
    hi = x.astype(BF16)
    return hi, (x - hi.astype(F32)).astype(BF16)


def dot_nn(a, b):
    left = jnp.concatenate([a[0], a[0], a[1]], axis=1)
    right = jnp.concatenate([b[0], b[1], b[0]], axis=0)
    return lax.dot_general(left, right, (((1,), (0,)), ((), ())), preferred_element_type=F32)


def dot_nt(a, b):
    left = jnp.concatenate([a[0], a[0], a[1]], axis=1)
    right = jnp.concatenate([b[0], b[1], b[0]], axis=1)
    return lax.dot_general(left, right, (((1,), (1,)), ((), ())), preferred_element_type=F32)


def call(kernel, out_shape, *, grid=(1,), scalars=0, in_specs, out_specs, scratch=(), flops=0, nbytes=0, aliases=None, mib=12):
    return pl.pallas_call(
        kernel,
        out_shape=out_shape,
        grid_spec=pltpu.PrefetchScalarGridSpec(
            num_scalar_prefetch=scalars, grid=grid, in_specs=in_specs, out_specs=out_specs, scratch_shapes=scratch
        ),
        compiler_params=pltpu.CompilerParams(vmem_limit_bytes=mib * MIB),
        cost_estimate=pl.CostEstimate(flops=flops, bytes_accessed=nbytes, transcendentals=0),
        input_output_aliases=aliases or {},
    )


def whole(shape):
    return pl.BlockSpec(shape, lambda *_: (0,) * len(shape))


def rows_at(chunk, width):
    return pl.BlockSpec((chunk, width), lambda s, *_: (s, 0))


def sds(shape, dtype=F32):
    return jax.ShapeDtypeStruct(shape, dtype)


def mask_roots(states, scal, pieces):
    roots, cap, width = states.shape
    step = cap // sum(TWIN)

    def kernel(s_ref, states_ref, own_ref, own_hi, own_lo, other_hi, other_lo, *other_refs):
        row = lax.broadcasted_iota(jnp.int32, (step, width), 0) + pl.program_id(0) * step
        col = lax.broadcasted_iota(jnp.int32, (step, width), 1)
        keep = (row < s_ref[1]) & (col < s_ref[2])
        own = jnp.where(keep, states_ref[s_ref[0]], 0.0)
        own_ref[...] = own
        own_hi[...], own_lo[...] = split(own)
        other = jnp.where(keep, states_ref[1 - s_ref[0]], 0.0)
        other_hi[...], other_lo[...] = split(other)
        first = 0
        for part, ref in zip(TWIN, other_refs):

            @pl.when((pl.program_id(0) >= first) & (pl.program_id(0) < first + part))
            def _():
                ref[...] = other

            first += part

    piece_specs, first = [], 0
    for part in TWIN:
        piece_specs.append(pl.BlockSpec((step, width), lambda s, *_, first=first, part=part: (jnp.clip(s - first, 0, part - 1), 0)))
        first += part
    half = sds((cap, width), BF16)
    own, own_hi, own_lo, other_hi, other_lo, *others = call(
        kernel,
        (sds((cap, width)), half, half, half, half) + tuple(sds((rows, width)) for rows in pieces),
        grid=(sum(TWIN),),
        scalars=1,
        in_specs=[pl.BlockSpec((roots, step, width), lambda s, *_: (0, s, 0))],
        out_specs=(rows_at(step, width),) * 5 + tuple(piece_specs),
        nbytes=4 * states.size * 3,
    )(scal, states)
    return own, (own_hi, own_lo), others, (other_hi, other_lo)


def fetched(kernel, inputs, buffers, outs, results, *, scalars, root=None, passed=(), extra=(), aliases=None, flops=0, mib):
    n_in, n_out = len(inputs), len(outs)
    laid = [k for k, (_, fills) in enumerate(buffers) if len(fills) > 1]
    direct = {k for k, _ in passed}

    def body(s_ref, *refs):
        ins, out_refs, refs = refs[:n_in], refs[n_in : n_in + n_out], refs[n_in + n_out :]
        bufs = dict(zip([k for k in laid if k not in direct], refs))
        rest = refs[len(bufs) :]
        for k, dst in passed:
            bufs[k] = out_refs[dst]

        def lay(k):
            for src, first, rows, to in buffers[k][1]:
                to = pl.multiple_of(to(s_ref), 8) if callable(to) else to
                bufs[k][pl.ds(to, rows), :] = ins[src][pl.ds(first, rows), :]

        def get(k):
            if k not in bufs:
                return ins[buffers[k][1][0][0]][...]
            lay(k)
            return bufs[k][...]

        def put(k, value):
            at = 0
            for dst in results[k][1]:
                rows = outs[dst].shape[-2]
                if root is None:
                    out_refs[dst][...] = value[at : at + rows]
                else:
                    out_refs[dst][0] = value
                at += rows

        def pass_on():
            for k, _ in passed:
                lay(k)

        kernel(get, put, pass_on, s_ref, *rest)

    scratch = [pltpu.VMEM(buffers[k][0], inputs[buffers[k][1][0][0]].dtype) for k in laid if k not in direct]
    used = {fill[0] for _, fills in buffers for fill in fills}
    in_specs = [whole(x.shape) if k in used else pl.BlockSpec(memory_space=pl.ANY) for k, x in enumerate(inputs)]
    if root is None:
        out_specs = tuple(whole(x.shape) for x in outs)
    else:
        out_specs = tuple(pl.BlockSpec((1, *x.shape[1:]), lambda s, s_ref: (root(s_ref), 0, 0)) for x in outs)
    return call(
        body,
        tuple(outs),
        scalars=1,
        in_specs=in_specs,
        out_specs=out_specs,
        scratch=scratch + list(extra),
        flops=flops,
        nbytes=sum(x.size * 4 for x in (*inputs, *outs)),
        aliases=aliases,
        mib=mib,
    )(scalars, *inputs)


class Operands:
    def __init__(self):
        self.inputs = []

    def add(self, array):
        for k, known in enumerate(self.inputs):
            if known is array:
                return k
        self.inputs.append(array)
        return len(self.inputs) - 1

    def stacked(self, *arrays):
        fills, at = [], 0
        for array in arrays:
            fills.append((self.add(array), 0, array.shape[0], at))
            at += array.shape[0]
        return (at, arrays[0].shape[1]), fills

    def placed(self, arrays, unit, first_scalar):
        fills = []
        for array in arrays:
            for sub in range(array.shape[0] // unit):
                at = first_scalar + len(fills)
                fills.append((self.add(array), sub * unit, unit, lambda s_ref, at=at: s_ref[at]))
        return (unit * len(fills), arrays[0].shape[1]), fills


def masked(value, s_ref):
    row = lax.broadcasted_iota(jnp.int32, value.shape, 0)
    col = lax.broadcasted_iota(jnp.int32, value.shape, 1)
    return jnp.where((row < s_ref[1]) & (col < s_ref[2]), value, 0.0)


def hub_out(scal, at_l, pieces, up, own, op_r, next_parts, lo_parts):
    cap, width = up.shape
    n = len(pieces)
    ops = Operands()
    buffers = [
        ops.stacked(op_r),
        ops.stacked(own[0]),
        ops.stacked(own[1]),
        ops.placed(lo_parts, lo_parts[0].shape[0], at_l),
        ops.stacked(up),
        ops.placed(next_parts, next_parts[0].shape[0], at_l),
    ]

    def kernel(get, put, pass_on, s_ref, mid):
        r = split(get(0))
        mid[0], mid[1] = split(dot_nn((get(1), get(2)), r))
        put(0, dot_nn(split(get(3).T), (mid[0], mid[1])))
        mid[2], mid[3] = split(dot_nt(split(get(4)), r))
        put(1, dot_nn(split(get(5)), (mid[2], mid[3])))

    got = fetched(
        kernel,
        ops.inputs,
        buffers,
        [sds((rows, width)) for rows in pieces] * 2,
        [((cap, width), list(range(n))), ((cap, width), list(range(n, 2 * n)))],
        scalars=scal,
        extra=[pltpu.VMEM((4, cap, width), BF16)],
        flops=24 * cap * cap * width,
        mib=30,
    )
    return got[n:], got[:n]


def joined(scal, parts, at=None, unit=None):
    ops = Operands()
    buffers = [ops.stacked(*parts) if at is None else ops.placed(parts, unit, at)]
    return fetched(
        lambda get, put, pass_on, s_ref: pass_on(),
        ops.inputs,
        buffers,
        [sds(buffers[0][0])],
        [],
        scalars=scal,
        passed=[(0, 0)],
        mib=8,
    )[0]


def right_product(scal, piece, op_r):
    ops = Operands()
    buffers = [ops.stacked(op_r), ops.stacked(piece)]

    def kernel(get, put, pass_on, s_ref):
        put(0, dot_nn(split(get(1)), split(get(0))))

    return fetched(
        kernel,
        ops.inputs,
        buffers,
        [sds(piece.shape)],
        [(piece.shape, [0])],
        scalars=scal,
        flops=6 * piece.size * piece.shape[1],
        mib=16,
    )[0]


def hub_own(scal, at_l, shape, hop_in, back_mid, op_r, lo_parts, next_parts, own_sum):
    _, cap, width = shape
    ops = Operands()
    buffers = [
        ops.stacked(op_r),
        ops.stacked(*hop_in),
        ops.stacked(*back_mid),
        ops.placed(lo_parts, lo_parts[0].shape[0], at_l),
        ops.placed(next_parts, next_parts[0].shape[0], at_l),
        ops.stacked(own_sum),
    ]

    def kernel(get, put, pass_on, s_ref, mid):
        mid[0], mid[1] = split(dot_nt(split(get(1)), split(get(0))))
        total = dot_nn(split(get(4).T), split(get(2))) + get(5)
        total = total + dot_nn(split(get(3)), (mid[0], mid[1]))
        put(0, masked(total, s_ref))

    return fetched(
        kernel,
        ops.inputs,
        buffers,
        [sds(shape)],
        [((cap, width), [0])],
        scalars=scal,
        root=lambda s_ref: s_ref[0],
        extra=[pltpu.VMEM((2, cap, width), BF16)],
        flops=18 * cap * cap * width,
        mib=30,
    )[0]


def left_local(scal, at_l, le_parts, own, other):
    cap, width = own[0].shape
    ops = Operands()
    buffers = [ops.placed(le_parts, le_parts[0].shape[0], at_l)] + [ops.stacked(x) for x in (*own, *other)]

    def kernel(get, put, pass_on, s_ref):
        a = split(get(0))
        put(0, dot_nn(a, (get(1), get(2))))
        put(1, dot_nn(a, (get(3), get(4))))

    return fetched(
        kernel,
        ops.inputs,
        buffers,
        [sds((cap, width))] * 2,
        [((cap, width), [k]) for k in range(2)],
        scalars=scal,
        flops=12 * cap * cap * width,
        mib=24,
    )


def right_local(scal, at_r, halves, unit, own, other, sums):
    cap, width = own[0].shape
    ops = Operands()
    buffers = [ops.placed(halves, unit, at_r)] + [ops.stacked(x) for x in (*own, *other, *sums)]

    def kernel(get, put, pass_on, s_ref):
        r = split(get(0))
        value = dot_nt((get(1), get(2)), r)
        put(0, get(5) + value)
        value = dot_nt((get(3), get(4)), r)
        put(1, get(6) + value)

    return fetched(
        kernel,
        ops.inputs,
        buffers,
        [sds((cap, width))] * 2,
        [((cap, width), [k]) for k in range(2)],
        scalars=scal,
        flops=12 * cap * width * width,
        mib=26,
    )


def combine(mine, hop, hop_far, back_far):
    def kernel(s_ref, a, b, c, out):
        out[...] = jnp.where(s_ref[0] == 0, a[...], b[...]) + c[...]

    return call(
        kernel,
        sds(hop.shape),
        scalars=1,
        in_specs=[whole(hop.shape)] * 3,
        out_specs=whole(hop.shape),
        nbytes=16 * hop.size,
    )(mine[None], hop, hop_far, back_far)


def finish(partial, scal, other_sum, returned):
    ops = Operands()
    buffers = [ops.stacked(other_sum), ops.stacked(*returned)]
    place = ops.add(partial)

    def kernel(get, put, pass_on, s_ref):
        total = get(0)
        put(0, masked(total + get(1), s_ref))

    return fetched(
        kernel,
        ops.inputs,
        buffers,
        [sds(partial.shape)],
        [(other_sum.shape, [0])],
        scalars=scal,
        root=lambda s_ref: 1 - s_ref[0],
        aliases={1 + place: 0},
        mib=12,
    )[0]


def on_device(n_l, n_r, states, left_env, right_env, left_op, right_op, sizes_left, sizes_right):
    cap = states.shape[1]
    i, j = lax.axis_index("lsec"), lax.axis_index("rsec")
    mine = (i % 2).astype(jnp.int32)
    sizes = (sizes_left[0], sizes_right[0])

    def move(value, to):
        pairs = []
        for a in range(n_l):
            for b in range(n_r):
                goal = to(a, b)
                if goal is not None and 0 <= goal[0] < n_l and 0 <= goal[1] < n_r:
                    pairs.append((a * n_r + b, goal[0] * n_r + goal[1]))
        return lax.ppermute(value, AXES, pairs)

    def swap(value):
        return move(value, lambda a, b: (a ^ 1, b))

    def spread_left(shard):
        held = {0: shard}
        bit = n_r // 2
        while bit:
            for m in list(held):
                held[m ^ bit] = move(held[m], lambda a, b: (a, b ^ bit))
            bit //= 2
        return held

    def spread_right(shard):
        return [shard] + [move(shard, lambda a, b: ((a + 2 * k) % n_l, b)) for k in range(1, n_l // 2)]

    lo, le = left_op[0], left_env[0]
    ro, re = right_op[0], right_env[0]
    rows_l, rows_r = lo.shape[0], ro.shape[0]

    def right_rows(base):
        return [((base - 2 * k) % n_l) * rows_r for k in range(n_l // 2)]

    next_lo = move(lo, lambda a, b: (a - 1, b))
    all_lo, all_le, all_n = spread_left(lo), spread_left(le), spread_left(next_lo)
    keys = list(all_lo)
    all_lo, all_le, all_n = ([held[m] for m in keys] for held in (all_lo, all_le, all_n))
    left_rows = [(j ^ m) * rows_l for m in keys]
    own_rows, twin_rows = right_rows(i), right_rows(i ^ 1)
    paired = [row for pair in zip(own_rows, twin_rows) for row in pair]
    scal = jnp.stack([mine, *sizes, *left_rows, *own_rows, *twin_rows, *paired]).astype(jnp.int32)
    at_l, at_r, at_e = 3, 3 + n_r, 3 + n_r + n_l

    twin_pieces = [cap * part // sum(TWIN) for part in TWIN]
    own, own_split, other, other_split = mask_roots(states, scal, twin_pieces)
    twin = [swap(piece) for piece in other]
    half_r = joined(scal, spread_right(ro))
    all_e = spread_right(joined(scal, [re, swap(re)]))
    up = move(own, lambda a, b: (a, b - 1))
    op_r = joined(scal, [half_r, swap(half_r)], at_r, rows_r)
    twin_hop = [move(v, lambda a, b: (a if a % 2 else a + 2, b - 1)) for v in twin]
    twin_mid = [right_product(scal, v, op_r) for v in twin]
    twin_mid = [move(v, lambda a, b: (a - 2 if a % 2 else a, b + 1)) for v in twin_mid]

    pieces = [cap * part // sum(RETURNS) for part in RETURNS]
    hops, backs = hub_out(scal, at_l, pieces, up, own_split, op_r, all_n, all_lo)
    returned = []
    for hop, back in zip(hops, backs):
        hop_far = move(hop, lambda a, b: (a + 2, b) if a % 2 else None)
        back_far = move(back, lambda a, b: (a if a % 2 else a - 2, b + 1))
        returned.append(swap(combine(mine, hop, hop_far, back_far)))

    sums = left_local(scal, at_l, all_le, own_split, other_split)
    own_sum, other_sum = right_local(scal, at_e, all_e, rows_r, own_split, other_split, sums)
    partial = hub_own(scal, at_l, states.shape, twin_hop, twin_mid, op_r, all_lo, all_n, own_sum)
    return finish(partial, scal, other_sum, returned)


def solution(mesh):
    in_specs = (
        P(None, "lsec", "rsec"),
        P("lsec", "rsec", None),
        P("rsec", "lsec", None),
        P("lsec", "rsec", None),
        P("rsec", "lsec", None),
        P("lsec"),
        P("rsec"),
    )
    n_l, n_r = mesh.shape["lsec"], mesh.shape["rsec"]

    def body(*args):
        return on_device(n_l, n_r, *args)

    return jax.shard_map(
        body, mesh=mesh, in_specs=in_specs, out_specs=P(None, "lsec", "rsec"), check_vma=False
    )
```

profile of v0, /device:TPU:11, one launch (start us, length us, event | category | flops | bytes accessed | tf_op | source)
XLA Modules:
  0.0 173.1 jit_solution(12286973319408378067)
XLA Ops:
  5.2 2.6 %collective-permute-start.14 = (f32[640,640]{1,0:T(8,128)S(1)}, f32[640,640]{1,0:T(8,128)S(1)}, u32[]{:S(2)}, u32[]{:S(2)}) collective-permute-start(f32[640,640]{1,0:T(8,128)S(1)} %get-tuple-element.29), channel_id=1, source_target_pairs={{1,0},{2,1},{3,2},{5,4},{6,5},{7,6},{9,8},{10,9},{11,10},{13,12},{... | collective-permute-start | bytes 4915208 | tf_op jit(solution)/shard_map/ppermute | solution.py:384
  11.9 2.9 %collective-permute-done.refs_1_ = f32[80,640]{1,0:T(8,128)S(1)} collective-permute-done((f32[80,640]{1,0:T(8,128)S(1)}, f32[80,640]{1,0:T(8,128)S(1)}, u32[]{:S(2)}, u32[]{:S(2)}) %collective-permute-start) | collective-permute-done | bytes 204832 | tf_op jit(solution)/shard_map/ppermute | solution.py:384
  17.0 10.4 %collective-permute-done.8.refs_2_ = f32[80,640]{1,0:T(8,128)S(1)} collective-permute-done((f32[80,640]{1,0:T(8,128)S(1)}, f32[80,640]{1,0:T(8,128)S(1)}, u32[]{:S(2)}, u32[]{:S(2)}) %collective-permute-start.8) | collective-permute-done | bytes 204832 | tf_op jit(solution)/shard_map/ppermute | solution.py:384
  29.1 3.3 %collective-permute-start.15 = (f32[160,640]{1,0:T(8,128)S(1)}, f32[160,640]{1,0:T(8,128)S(1)}, u32[]{:S(2)}, u32[]{:S(2)}) collective-permute-start(f32[160,640]{1,0:T(8,128)S(1)} %bitcast.27), channel_id=1, source_target_pairs={{4,0},{5,1},{6,2},{7,3},{8,4},{9,5},{10,6},{11,7},{12,8},{13,9},{1... | collective-permute-start | bytes 1228808 | tf_op jit(solution)/shard_map/ppermute | solution.py:384
  32.3 9.2 %collective-permute-start.12 = (f32[160,640]{1,0:T(8,128)S(1)}, f32[160,640]{1,0:T(8,128)S(1)}, u32[]{:S(2)}, u32[]{:S(2)}) collective-permute-start(f32[160,640]{1,0:T(8,128)S(1)} %bitcast.28), channel_id=1, source_target_pairs={{0,1},{1,0},{2,3},{3,2},{4,5},{5,4},{6,7},{7,6},{8,9},{9,8},{10,11... | collective-permute-start | bytes 1228808 | tf_op jit(solution)/shard_map/ppermute | solution.py:384
  44.4 3.2 %collective-permute-start.13 = (f32[160,640]{1,0:T(8,128)S(1)}, f32[160,640]{1,0:T(8,128)S(1)}, u32[]{:S(2)}, u32[]{:S(2)}) collective-permute-start(f32[160,640]{1,0:T(8,128)S(1)} %collective-permute-done.11.refs_4_.refs_6_), channel_id=1, source_target_pairs={{0,1},{1,0},{2,3},{3,2},{4,5},{5,4},{6,7},{7,6},{8,9},{9,8},{10,11... | collective-permute-start | bytes 1228808 | tf_op jit(solution)/shard_map/ppermute | solution.py:384
  47.6 3.7 %collective-permute-done.1.refs_1_ = f32[160,640]{1,0:T(8,128)S(1)} collective-permute-done((f32[160,640]{1,0:T(8,128)S(1)}, f32[160,640]{1,0:T(8,128)S(1)}, u32[]{:S(2)}, u32[]{:S(2)}) %collective-permute-start.1) | collective-permute-done | bytes 409632 | tf_op jit(solution)/shard_map/ppermute | solution.py:384
  51.3 3.7 %collective-permute-start.17 = (f32[160,640]{1,0:T(8,128)S(1)}, f32[160,640]{1,0:T(8,128)S(1)}, u32[]{:S(2)}, u32[]{:S(2)}) collective-permute-start(f32[160,640]{1,0:T(8,128)S(1)} %collective-permute-done.15.refs_8_.refs_9_), channel_id=1, source_target_pairs={{0,1},{1,0},{2,3},{3,2},{4,5},{5,4},{6,7},{7,6},{8,9},{9,8},{10,11... | collective-permute-start | bytes 1228808 | tf_op jit(solution)/shard_map/ppermute | solution.py:384
  57.5 4.5 %collective-permute-done.10.refs_1_ = f32[320,640]{1,0:T(8,128)S(1)} collective-permute-done((f32[320,640]{1,0:T(8,128)S(1)}, f32[320,640]{1,0:T(8,128)S(1)}, u32[]{:S(2)}, u32[]{:S(2)}) %collective-permute-start.10) | collective-permute-done | bytes 819232 | tf_op jit(solution)/shard_map/ppermute | solution.py:384
  62.9 2.4 %collective-permute-start.2 = (f32[160,640]{1,0:T(8,128)S(1)}, f32[160,640]{1,0:T(8,128)S(1)}, u32[]{:S(2)}, u32[]{:S(2)}) collective-permute-start(f32[160,640]{1,0:T(8,128)S(1)} %shard_map.73.refs_0_), channel_id=1, source_target_pairs={{0,16},{1,17},{2,18},{3,19},{4,20},{5,21},{6,22},{7,23},{8,24},{9,... | collective-permute-start | bytes 1228808 | tf_op jit(solution)/shard_map/ppermute | solution.py:384
  67.7 9.0 %shard_map.79 = (f32[256,640]{1,0:T(8,128)S(1)}, f32[256,640]{1,0:T(8,128)S(1)}, f32[128,640]{1,0:T(8,128)S(1)}, f32[256,640]{1,0:T(8,128)S(1)}, f32[256,640]{1,0:T(8,128)S(1)}, /*index=5*/f32[128,640]{1,0:T(8,128)S(1)}) custom-call(s32[23]{0:T(128)S(1)} %stack.63.s_ref, f32[640,640]{1,0:T(8,128)S(1)} %shard_map.78.refs_0_, ...), custom_call_target="tpu_custom_call" | custom-call | flops 6291456000 | bytes 13107200 | tf_op jit(solution)/shard_map/pallas_call | solution.py:142
  76.6 2.6 %collective-permute-start.29 = (f32[256,640]{1,0:T(8,128)S(1)}, f32[256,640]{1,0:T(8,128)S(1)}, u32[]{:S(2)}, u32[]{:S(2)}) collective-permute-start(f32[256,640]{1,0:T(8,128)S(1)} %collective-permute-done.28.refs_1_), channel_id=1, source_target_pairs={{1,8},{2,9},{3,10},{5,4},{6,5},{7,6},{9,16},{10,17},{11,18},{13,12... | collective-permute-start | bytes 1966088 | tf_op jit(solution)/shard_map/ppermute | solution.py:384
  79.3 12.7 %collective-permute-done.2.refs_2_ = f32[160,640]{1,0:T(8,128)S(1)} collective-permute-done((f32[160,640]{1,0:T(8,128)S(1)}, f32[160,640]{1,0:T(8,128)S(1)}, u32[]{:S(2)}, u32[]{:S(2)}) %collective-permute-start.2) | collective-permute-done | bytes 409632 | tf_op jit(solution)/shard_map/ppermute | solution.py:384
  95.8 5.3 %collective-permute-start.22 = (f32[256,640]{1,0:T(8,128)S(1)}, f32[256,640]{1,0:T(8,128)S(1)}, u32[]{:S(2)}, u32[]{:S(2)}) collective-permute-start(f32[256,640]{1,0:T(8,128)S(1)} %get-tuple-element.32.a), channel_id=1, source_target_pairs={{4,12},{5,13},{6,14},{7,15},{12,20},{13,21},{14,22},{15,23},{20,28... | collective-permute-start | bytes 1966088 | tf_op jit(solution)/shard_map/ppermute | solution.py:384
  105.2 2.2 %collective-permute-start.31 = (f32[384,640]{1,0:T(8,128)S(1)}, f32[384,640]{1,0:T(8,128)S(1)}, u32[]{:S(2)}, u32[]{:S(2)}) collective-permute-start(f32[384,640]{1,0:T(8,128)S(1)} %collective-permute-done.30.refs_1_), channel_id=1, source_target_pairs={{1,8},{2,9},{3,10},{5,4},{6,5},{7,6},{9,16},{10,17},{11,18},{13,12... | collective-permute-start | bytes 2949128 | tf_op jit(solution)/shard_map/ppermute | solution.py:384
  109.6 2.3 %collective-permute-start.33 = (f32[384,640]{1,0:T(8,128)S(1)}, f32[384,640]{1,0:T(8,128)S(1)}, u32[]{:S(2)}, u32[]{:S(2)}) collective-permute-start(f32[384,640]{1,0:T(8,128)S(1)} %shard_map.84), channel_id=1, source_target_pairs={{0,1},{1,2},{2,3},{8,9},{9,10},{10,11},{12,5},{13,6},{14,7},{16,17... | collective-permute-start | bytes 2949128 | tf_op jit(solution)/shard_map/ppermute | solution.py:384
  115.5 8.2 %collective-permute-done.22.b = f32[256,640]{1,0:T(8,128)S(1)} collective-permute-done((f32[256,640]{1,0:T(8,128)S(1)}, f32[256,640]{1,0:T(8,128)S(1)}, u32[]{:S(2)}, u32[]{:S(2)}) %collective-permute-start.22) | collective-permute-done | bytes 655392 | tf_op jit(solution)/shard_map/ppermute | solution.py:384
  123.7 3.1 %collective-permute-start.25 = (f32[128,640]{1,0:T(8,128)S(1)}, f32[128,640]{1,0:T(8,128)S(1)}, u32[]{:S(2)}, u32[]{:S(2)}) collective-permute-start(f32[128,640]{1,0:T(8,128)S(1)} %get-tuple-element.34.a), channel_id=1, source_target_pairs={{4,12},{5,13},{6,14},{7,15},{12,20},{13,21},{14,22},{15,23},{20,28... | collective-permute-start | bytes 983048 | tf_op jit(solution)/shard_map/ppermute | solution.py:384
  126.8 2.9 %collective-permute-start.26 = (f32[128,640]{1,0:T(8,128)S(1)}, f32[128,640]{1,0:T(8,128)S(1)}, u32[]{:S(2)}, u32[]{:S(2)}) collective-permute-start(f32[128,640]{1,0:T(8,128)S(1)} %get-tuple-element.35), channel_id=1, source_target_pairs={{4,5},{5,6},{6,7},{8,1},{9,2},{10,3},{12,13},{13,14},{14,15},{16,9... | collective-permute-start | bytes 983048 | tf_op jit(solution)/shard_map/ppermute | solution.py:384
  129.6 4.8 %shard_map.75 = (f32[640,640]{1,0:T(8,128)S(1)}, f32[640,640]{1,0:T(8,128)S(1)}) custom-call(s32[23]{0:T(128)S(1)} %stack.63.s_ref, f32[160,640]{1,0:T(8,128)S(1)} %bitcast.25, f32[160,640]{1,0:T(8,128)S(1)} %collective-permute-done.4.refs_1_, f32[160,640]{1,0:T(8,128)S(1)} %collective-permute-done.5.refs_2_, f32[160,640]{1,0:T(8,128)S(1)} %collective-permute-done.6.refs_3_, ...), custom_call_target="tpu_custom_call" | custom-call | flops 3145728000 | bytes 11468800 | tf_op jit(solution)/shard_map/pallas_call | solution.py:142
  137.5 4.9 %shard_map.76 = (f32[640,640]{1,0:T(8,128)S(1)}, f32[640,640]{1,0:T(8,128)S(1)}) custom-call(s32[23]{0:T(128)S(1)} %stack.63.s_ref, f32[160,640]{1,0:T(8,128)S(1)} %shard_map.73.refs_0_, f32[160,640]{1,0:T(8,128)S(1)} %collective-permute-done.1.refs_1_, f32[160,640]{1,0:T(8,128)S(1)} %collective-permute-done.2.refs_2_, ...), custom_call_target="tpu_custom_call" | custom-call | flops 3145728000 | bytes 14745600 | tf_op jit(solution)/shard_map/pallas_call | solution.py:142
  142.4 8.1 %collective-permute-done.32.refs_3_ = f32[256,640]{1,0:T(8,128)S(1)} collective-permute-done((f32[256,640]{1,0:T(8,128)S(1)}, f32[256,640]{1,0:T(8,128)S(1)}, u32[]{:S(2)}, u32[]{:S(2)}) %collective-permute-start.32) | collective-permute-done | bytes 655392 | tf_op jit(solution)/shard_map/ppermute | solution.py:384
  150.5 8.2 %shard_map.85.refs_4_ = f32[2,640,640]{2,1,0:T(8,128)} custom-call(s32[23]{0:T(128)S(1)} %stack.63.s_ref, f32[640,640]{1,0:T(8,128)S(1)} %shard_map.78.refs_0_, f32[256,640]{1,0:T(8,128)S(1)} %collective-permute-done.29.refs_1_, f32[384,640]{1,0:T(8,128)S(1)} %collective-permute-done.31.refs_2_, f32[256,640]{1,0:T(8,128)S(1)} %collective-permute-done.32.refs_3_, ...), custom_call_target="tpu_custom_call" | custom-call | flops 4718592000 | bytes 13107200 | tf_op jit(solution)/shard_map/pallas_call | solution.py:142
  158.7 12.5 %collective-permute-done.27.refs_3_ = f32[128,640]{1,0:T(8,128)S(1)} collective-permute-done((f32[128,640]{1,0:T(8,128)S(1)}, f32[128,640]{1,0:T(8,128)S(1)}, u32[]{:S(2)}, u32[]{:S(2)}) %collective-permute-start.27) | collective-permute-done | bytes 327712 | tf_op jit(solution)/shard_map/ppermute | solution.py:384
  (69 shorter events, 38.9 us)
Async XLA Ops:
  5.2 60.3 %collective-permute-start.14 = (f32[640,640]{1,0:T(8,128)S(1)}, f32[640,640]{1,0:T(8,128)S(1)}, u32[]{:S(2)}, u32[]{:S(2)}) collective-permute-start(f32[640,640]{1,0:T(8,128)S(1)} %get-tuple-element.29), channel_id=1, source_target_pairs={{1,0},{2,1},{3,2},{5,4},{6,5},{7,6},{9,8},{10,9},{11,10},{13,12},{... | collective-permute-start | bytes 4915208 | tf_op jit(solution)/shard_map/ppermute | solution.py:384
  9.4 17.9 %collective-permute-start.8 = (f32[80,640]{1,0:T(8,128)S(1)}, f32[80,640]{1,0:T(8,128)S(1)}, u32[]{:S(2)}, u32[]{:S(2)}) collective-permute-start(f32[80,640]{1,0:T(8,128)S(1)} %bitcast.18), channel_id=1, source_target_pairs={{0,16},{1,17},{2,18},{3,19},{4,20},{5,21},{6,22},{7,23},{8,24},{9,... | collective-permute-start | bytes 614408 | tf_op jit(solution)/shard_map/ppermute | solution.py:384
  10.4 18.6 %collective-permute-start.9 = (f32[80,640]{1,0:T(8,128)S(1)}, f32[80,640]{1,0:T(8,128)S(1)}, u32[]{:S(2)}, u32[]{:S(2)}) collective-permute-start(f32[80,640]{1,0:T(8,128)S(1)} %bitcast.19), channel_id=1, source_target_pairs={{0,24},{1,25},{2,26},{3,27},{4,28},{5,29},{6,30},{7,31},{8,0},{9,1... | collective-permute-start | bytes 614408 | tf_op jit(solution)/shard_map/ppermute | solution.py:384
  14.8 17.5 %collective-permute-start.4 = (f32[160,640]{1,0:T(8,128)S(1)}, f32[160,640]{1,0:T(8,128)S(1)}, u32[]{:S(2)}, u32[]{:S(2)}) collective-permute-start(f32[160,640]{1,0:T(8,128)S(1)} %bitcast.23), channel_id=1, source_target_pairs={{0,2},{1,3},{2,0},{3,1},{4,6},{5,7},{6,4},{7,5},{8,10},{9,11},{10,... | collective-permute-start | bytes 1228808 | tf_op jit(solution)/shard_map/ppermute | solution.py:384
  15.9 26.2 %collective-permute-start.5 = (f32[160,640]{1,0:T(8,128)S(1)}, f32[160,640]{1,0:T(8,128)S(1)}, u32[]{:S(2)}, u32[]{:S(2)}) collective-permute-start(f32[160,640]{1,0:T(8,128)S(1)} %bitcast.24), channel_id=1, source_target_pairs={{0,1},{1,0},{2,3},{3,2},{4,5},{5,4},{6,7},{7,6},{8,9},{9,8},{10,11... | collective-permute-start | bytes 1228808 | tf_op jit(solution)/shard_map/ppermute | solution.py:384
  27.3 15.7 %collective-permute-start.11 = (f32[160,640]{1,0:T(8,128)S(1)}, f32[160,640]{1,0:T(8,128)S(1)}, u32[]{:S(2)}, u32[]{:S(2)}) collective-permute-start(f32[160,640]{1,0:T(8,128)S(1)} %bitcast.26), channel_id=1, source_target_pairs={{0,2},{1,3},{2,0},{3,1},{4,6},{5,7},{6,4},{7,5},{8,10},{9,11},{10,... | collective-permute-start | bytes 1228808 | tf_op jit(solution)/shard_map/ppermute | solution.py:384
  29.1 15.3 %collective-permute-start.15 = (f32[160,640]{1,0:T(8,128)S(1)}, f32[160,640]{1,0:T(8,128)S(1)}, u32[]{:S(2)}, u32[]{:S(2)}) collective-permute-start(f32[160,640]{1,0:T(8,128)S(1)} %bitcast.27), channel_id=1, source_target_pairs={{4,0},{5,1},{6,2},{7,3},{8,4},{9,5},{10,6},{11,7},{12,8},{13,9},{1... | collective-permute-start | bytes 1228808 | tf_op jit(solution)/shard_map/ppermute | solution.py:384
  42.2 19.9 %collective-permute-start.10 = (f32[320,640]{1,0:T(8,128)S(1)}, f32[320,640]{1,0:T(8,128)S(1)}, u32[]{:S(2)}, u32[]{:S(2)}) collective-permute-start(f32[320,640]{1,0:T(8,128)S(1)} %shard_map.77.refs_0_), channel_id=1, source_target_pairs={{0,4},{1,5},{2,6},{3,7},{4,0},{5,1},{6,2},{7,3},{8,12},{9,13},{10,... | collective-permute-start | bytes 2457608 | tf_op jit(solution)/shard_map/ppermute | solution.py:384
  56.3 20.3 %collective-permute-start.28 = (f32[256,640]{1,0:T(8,128)S(1)}, f32[256,640]{1,0:T(8,128)S(1)}, u32[]{:S(2)}, u32[]{:S(2)}) collective-permute-start(f32[256,640]{1,0:T(8,128)S(1)} %get-tuple-element.36), channel_id=1, source_target_pairs={{0,4},{1,5},{2,6},{3,7},{4,0},{5,1},{6,2},{7,3},{8,12},{9,13},{10,... | collective-permute-start | bytes 1966088 | tf_op jit(solution)/shard_map/ppermute | solution.py:384
  62.0 39.1 %collective-permute-start.30 = (f32[384,640]{1,0:T(8,128)S(1)}, f32[384,640]{1,0:T(8,128)S(1)}, u32[]{:S(2)}, u32[]{:S(2)}) collective-permute-start(f32[384,640]{1,0:T(8,128)S(1)} %get-tuple-element.37), channel_id=1, source_target_pairs={{0,4},{1,5},{2,6},{3,7},{4,0},{5,1},{6,2},{7,3},{8,12},{9,13},{10,... | collective-permute-start | bytes 2949128 | tf_op jit(solution)/shard_map/ppermute | solution.py:384
  62.9 29.0 %collective-permute-start.2 = (f32[160,640]{1,0:T(8,128)S(1)}, f32[160,640]{1,0:T(8,128)S(1)}, u32[]{:S(2)}, u32[]{:S(2)}) collective-permute-start(f32[160,640]{1,0:T(8,128)S(1)} %shard_map.73.refs_0_), channel_id=1, source_target_pairs={{0,16},{1,17},{2,18},{3,19},{4,20},{5,21},{6,22},{7,23},{8,24},{9,... | collective-permute-start | bytes 1228808 | tf_op jit(solution)/shard_map/ppermute | solution.py:384
  65.3 28.5 %collective-permute-start.3 = (f32[160,640]{1,0:T(8,128)S(1)}, f32[160,640]{1,0:T(8,128)S(1)}, u32[]{:S(2)}, u32[]{:S(2)}) collective-permute-start(f32[160,640]{1,0:T(8,128)S(1)} %shard_map.73.refs_0_), channel_id=1, source_target_pairs={{0,24},{1,25},{2,26},{3,27},{4,28},{5,29},{6,30},{7,31},{8,0},{9,1... | collective-permute-start | bytes 1228808 | tf_op jit(solution)/shard_map/ppermute | solution.py:384
  65.5 30.3 %collective-permute-start.6 = (f32[160,640]{1,0:T(8,128)S(1)}, f32[160,640]{1,0:T(8,128)S(1)}, u32[]{:S(2)}, u32[]{:S(2)}) collective-permute-start(f32[160,640]{1,0:T(8,128)S(1)} %collective-permute-done.4.refs_1_), channel_id=1, source_target_pairs={{0,1},{1,0},{2,3},{3,2},{4,5},{5,4},{6,7},{7,6},{8,9},{9,8},{10,11... | collective-permute-start | bytes 1228808 | tf_op jit(solution)/shard_map/ppermute | solution.py:384
  76.6 28.5 %collective-permute-start.29 = (f32[256,640]{1,0:T(8,128)S(1)}, f32[256,640]{1,0:T(8,128)S(1)}, u32[]{:S(2)}, u32[]{:S(2)}) collective-permute-start(f32[256,640]{1,0:T(8,128)S(1)} %collective-permute-done.28.refs_1_), channel_id=1, source_target_pairs={{1,8},{2,9},{3,10},{5,4},{6,5},{7,6},{9,16},{10,17},{11,18},{13,12... | collective-permute-start | bytes 1966088 | tf_op jit(solution)/shard_map/ppermute | solution.py:384
  91.9 17.7 %collective-permute-start.19 = (f32[256,640]{1,0:T(8,128)S(1)}, f32[256,640]{1,0:T(8,128)S(1)}, u32[]{:S(2)}, u32[]{:S(2)}) collective-permute-start(f32[256,640]{1,0:T(8,128)S(1)} %get-tuple-element.30.a), channel_id=1, source_target_pairs={{4,12},{5,13},{6,14},{7,15},{12,20},{13,21},{14,22},{15,23},{20,28... | collective-permute-start | bytes 1966088 | tf_op jit(solution)/shard_map/ppermute | solution.py:384
  93.9 19.7 %collective-permute-start.20 = (f32[256,640]{1,0:T(8,128)S(1)}, f32[256,640]{1,0:T(8,128)S(1)}, u32[]{:S(2)}, u32[]{:S(2)}) collective-permute-start(f32[256,640]{1,0:T(8,128)S(1)} %get-tuple-element.31), channel_id=1, source_target_pairs={{4,5},{5,6},{6,7},{8,1},{9,2},{10,3},{12,13},{13,14},{14,15},{16,9... | collective-permute-start | bytes 1966088 | tf_op jit(solution)/shard_map/ppermute | solution.py:384
  95.8 27.9 %collective-permute-start.22 = (f32[256,640]{1,0:T(8,128)S(1)}, f32[256,640]{1,0:T(8,128)S(1)}, u32[]{:S(2)}, u32[]{:S(2)}) collective-permute-start(f32[256,640]{1,0:T(8,128)S(1)} %get-tuple-element.32.a), channel_id=1, source_target_pairs={{4,12},{5,13},{6,14},{7,15},{12,20},{13,21},{14,22},{15,23},{20,28... | collective-permute-start | bytes 1966088 | tf_op jit(solution)/shard_map/ppermute | solution.py:384
  101.1 25.7 %collective-permute-start.23 = (f32[256,640]{1,0:T(8,128)S(1)}, f32[256,640]{1,0:T(8,128)S(1)}, u32[]{:S(2)}, u32[]{:S(2)}) collective-permute-start(f32[256,640]{1,0:T(8,128)S(1)} %get-tuple-element.33), channel_id=1, source_target_pairs={{4,5},{5,6},{6,7},{8,1},{9,2},{10,3},{12,13},{13,14},{14,15},{16,9... | collective-permute-start | bytes 1966088 | tf_op jit(solution)/shard_map/ppermute | solution.py:384
  105.2 45.3 %collective-permute-start.31 = (f32[384,640]{1,0:T(8,128)S(1)}, f32[384,640]{1,0:T(8,128)S(1)}, u32[]{:S(2)}, u32[]{:S(2)}) collective-permute-start(f32[384,640]{1,0:T(8,128)S(1)} %collective-permute-done.30.refs_1_), channel_id=1, source_target_pairs={{1,8},{2,9},{3,10},{5,4},{6,5},{7,6},{9,16},{10,17},{11,18},{13,12... | collective-permute-start | bytes 2949128 | tf_op jit(solution)/shard_map/ppermute | solution.py:384
  109.6 40.9 %collective-permute-start.33 = (f32[384,640]{1,0:T(8,128)S(1)}, f32[384,640]{1,0:T(8,128)S(1)}, u32[]{:S(2)}, u32[]{:S(2)}) collective-permute-start(f32[384,640]{1,0:T(8,128)S(1)} %shard_map.84), channel_id=1, source_target_pairs={{0,1},{1,2},{2,3},{8,9},{9,10},{10,11},{12,5},{13,6},{14,7},{16,17... | collective-permute-start | bytes 2949128 | tf_op jit(solution)/shard_map/ppermute | solution.py:384
  113.5 37.0 %collective-permute-start.32 = (f32[256,640]{1,0:T(8,128)S(1)}, f32[256,640]{1,0:T(8,128)S(1)}, u32[]{:S(2)}, u32[]{:S(2)}) collective-permute-start(f32[256,640]{1,0:T(8,128)S(1)} %shard_map.83), channel_id=1, source_target_pairs={{0,1},{1,2},{2,3},{8,9},{9,10},{10,11},{12,5},{13,6},{14,7},{16,17... | collective-permute-start | bytes 1966088 | tf_op jit(solution)/shard_map/ppermute | solution.py:384
  134.7 36.5 %collective-permute-start.21 = (f32[256,640]{1,0:T(8,128)S(1)}, f32[256,640]{1,0:T(8,128)S(1)}, u32[]{:S(2)}, u32[]{:S(2)}) collective-permute-start(f32[256,640]{1,0:T(8,128)S(1)} %shard_map.80), channel_id=1, source_target_pairs={{0,4},{1,5},{2,6},{3,7},{4,0},{5,1},{6,2},{7,3},{8,12},{9,13},{10,... | collective-permute-start | bytes 1966088 | tf_op jit(solution)/shard_map/ppermute | solution.py:384
  136.8 34.4 %collective-permute-start.24 = (f32[256,640]{1,0:T(8,128)S(1)}, f32[256,640]{1,0:T(8,128)S(1)}, u32[]{:S(2)}, u32[]{:S(2)}) collective-permute-start(f32[256,640]{1,0:T(8,128)S(1)} %shard_map.81), channel_id=1, source_target_pairs={{0,4},{1,5},{2,6},{3,7},{4,0},{5,1},{6,2},{7,3},{8,12},{9,13},{10,... | collective-permute-start | bytes 1966088 | tf_op jit(solution)/shard_map/ppermute | solution.py:384
  150.5 20.7 %collective-permute-start.27 = (f32[128,640]{1,0:T(8,128)S(1)}, f32[128,640]{1,0:T(8,128)S(1)}, u32[]{:S(2)}, u32[]{:S(2)}) collective-permute-start(f32[128,640]{1,0:T(8,128)S(1)} %shard_map.82), channel_id=1, source_target_pairs={{0,4},{1,5},{2,6},{3,7},{4,0},{5,1},{6,2},{7,3},{8,12},{9,13},{10,... | collective-permute-start | bytes 983048 | tf_op jit(solution)/shard_map/ppermute | solution.py:384
  (15 other events, 147.0 us)
where the time goes:
time: 176 us; the launch traced here: 173 us
  waiting for transfers between devices  68.1 us (39%)
  starting transfers between devices  65.2 us (37%)
  Pallas kernels  36 us (20%)
  local copies, waits for them, and re-layouts  2.04 us (1%)
    ppermute x34, waiting for transfers between devices, move(): return lax.ppermute(value, AXES, pairs)  68.1 us
    ppermute x34, starting transfers between devices, move(): return lax.ppermute(value, AXES, pairs)  65.2 us
    pallas_call x10, Pallas kernels, fetched(): call(body, tuple(outs), scalars=1, in_specs=in_specs, out_specs=out_specs...  34 us
  transfers between devices with their start and end apart: 34, of which 11 were waited for; matrix products, arithmetic and copies ran while one was open for 0% of the time, Pallas kernels for 19%

commit v1 on v0

--- a/solution.py
+++ b/solution.py
@@ -254,23 +254,44 @@
     )[0]
 
 
-def hub_own(scal, at_l, shape, hop_in, back_mid, op_r, lo_parts, next_parts, own_sum):
-    _, cap, width = shape
+def own_hop(scal, at_l, hop_in, op_r, lo_parts, own_sum):
+    cap, width = own_sum.shape
     ops = Operands()
     buffers = [
         ops.stacked(op_r),
         ops.stacked(*hop_in),
+        ops.placed(lo_parts, lo_parts[0].shape[0], at_l),
+        ops.stacked(own_sum),
+    ]
+
+    def kernel(get, put, pass_on, s_ref, mid):
+        mid[0], mid[1] = split(dot_nt(split(get(1)), split(get(0))))
+        put(0, get(3) + dot_nn(split(get(2)), (mid[0], mid[1])))
+
+    return fetched(
+        kernel,
+        ops.inputs,
+        buffers,
+        [sds((cap, width))],
+        [((cap, width), [0])],
+        scalars=scal,
+        extra=[pltpu.VMEM((2, cap, width), BF16)],
+        flops=12 * cap * cap * width,
+        mib=26,
+    )[0]
+
+
+def own_back(scal, at_l, shape, back_mid, next_parts, own_sum):
+    _, cap, width = shape
+    ops = Operands()
+    buffers = [
         ops.stacked(*back_mid),
-        ops.placed(lo_parts, lo_parts[0].shape[0], at_l),
         ops.placed(next_parts, next_parts[0].shape[0], at_l),
         ops.stacked(own_sum),
     ]
 
-    def kernel(get, put, pass_on, s_ref, mid):
-        mid[0], mid[1] = split(dot_nt(split(get(1)), split(get(0))))
-        total = dot_nn(split(get(4).T), split(get(2))) + get(5)
-        total = total + dot_nn(split(get(3)), (mid[0], mid[1]))
-        put(0, masked(total, s_ref))
+    def kernel(get, put, pass_on, s_ref):
+        put(0, masked(dot_nn(split(get(1).T), split(get(0))) + get(2), s_ref))
 
     return fetched(
         kernel,
@@ -280,9 +301,8 @@
         [((cap, width), [0])],
         scalars=scal,
         root=lambda s_ref: s_ref[0],
-        extra=[pltpu.VMEM((2, cap, width), BF16)],
-        flops=18 * cap * cap * width,
-        mib=30,
+        flops=6 * cap * cap * width,
+        mib=24,
     )[0]
 
 
@@ -436,7 +456,8 @@
 
     sums = left_local(scal, at_l, all_le, own_split, other_split)
     own_sum, other_sum = right_local(scal, at_e, all_e, rows_r, own_split, other_split, sums)
-    partial = hub_own(scal, at_l, states.shape, twin_hop, twin_mid, op_r, all_lo, all_n, own_sum)
+    own_sum = own_hop(scal, at_l, twin_hop, op_r, all_lo, own_sum)
+    partial = own_back(scal, at_l, states.shape, twin_mid, all_n, own_sum)
     return finish(partial, scal, other_sum, returned)
 
 

time: 176 us -> 186 us (1.057); the launches traced: 173 us -> 185 us
  starting transfers between devices: 65.2 us -> 73.7 us
  waiting for transfers between devices: 68.1 us -> 70.7 us
    ppermute x34, starting transfers between devices: 65.2 us -> 73.7 us  [move(): return lax.ppermute(value, AXES, pairs)]
    ppermute x34, waiting for transfers between devices: 68.1 us -> 70.7 us  [move(): return lax.ppermute(value, AXES, pairs)]
    pallas_call x10 -> x11, Pallas kernels: 34 us -> 34.9 us  [fetched(): call(body, tuple(outs), scalars=1, in_specs=in_specs, out_specs=out_specs...]
  transfers between devices with their start and end apart: 34 -> 34, of which waited for: 11 -> 9; matrix products, arithmetic and copies ran while one was open for 0% -> 0% of each run, Pallas kernels for 19% -> 19%
where the time goes in v1:
time: 186 us; the launch traced here: 185 us
  starting transfers between devices  73.7 us (40%)
  waiting for transfers between devices  70.7 us (38%)
  Pallas kernels  36.9 us (20%)
  local copies, waits for them, and re-layouts  2.04 us (1%)
    ppermute x34, starting transfers between devices, move(): return lax.ppermute(value, AXES, pairs)  73.7 us
    ppermute x34, waiting for transfers between devices, move(): return lax.ppermute(value, AXES, pairs)  70.7 us
    pallas_call x11, Pallas kernels, fetched(): call(body, tuple(outs), scalars=1, in_specs=in_specs, out_specs=out_specs...  34.9 us
  transfers between devices with their start and end apart: 34, of which 9 were waited for; matrix products, arithmetic and copies ran while one was open for 0% of the time, Pallas kernels for 19%

profile of v1, /device:TPU:11, one launch (start us, length us, event | category | flops | bytes accessed | tf_op | source)
XLA Modules:
  0.0 185.1 jit_solution(3098157904210692977)
XLA Ops:
  8.9 3.8 %collective-permute-start.14 = (f32[640,640]{1,0:T(8,128)S(1)}, f32[640,640]{1,0:T(8,128)S(1)}, u32[]{:S(2)}, u32[]{:S(2)}) collective-permute-start(f32[640,640]{1,0:T(8,128)S(1)} %get-tuple-element.29), channel_id=1, source_target_pairs={{1,0},{2,1},{3,2},{5,4},{6,5},{7,6},{9,8},{10,9},{11,10},{13,12},{... | collective-permute-start | bytes 4915208 | tf_op jit(solution)/shard_map/ppermute | solution.py:404
  14.1 4.1 %collective-permute-start.9 = (f32[80,640]{1,0:T(8,128)S(1)}, f32[80,640]{1,0:T(8,128)S(1)}, u32[]{:S(2)}, u32[]{:S(2)}) collective-permute-start(f32[80,640]{1,0:T(8,128)S(1)} %bitcast.19), channel_id=1, source_target_pairs={{0,24},{1,25},{2,26},{3,27},{4,28},{5,29},{6,30},{7,31},{8,0},{9,1... | collective-permute-start | bytes 614408 | tf_op jit(solution)/shard_map/ppermute | solution.py:404
  18.3 3.9 %collective-permute-done.9.refs_3_ = f32[80,640]{1,0:T(8,128)S(1)} collective-permute-done((f32[80,640]{1,0:T(8,128)S(1)}, f32[80,640]{1,0:T(8,128)S(1)}, u32[]{:S(2)}, u32[]{:S(2)}) %collective-permute-start.9) | collective-permute-done | bytes 204832 | tf_op jit(solution)/shard_map/ppermute | solution.py:404
  23.6 3.1 %collective-permute-start.15 = (f32[160,640]{1,0:T(8,128)S(1)}, f32[160,640]{1,0:T(8,128)S(1)}, u32[]{:S(2)}, u32[]{:S(2)}) collective-permute-start(f32[160,640]{1,0:T(8,128)S(1)} %bitcast.28), channel_id=1, source_target_pairs={{4,0},{5,1},{6,2},{7,3},{8,4},{9,5},{10,6},{11,7},{12,8},{13,9},{1... | collective-permute-start | bytes 1228808 | tf_op jit(solution)/shard_map/ppermute | solution.py:404
  27.3 2.2 %collective-permute-start.10 = (f32[320,640]{1,0:T(8,128)S(1)}, f32[320,640]{1,0:T(8,128)S(1)}, u32[]{:S(2)}, u32[]{:S(2)}) collective-permute-start(f32[320,640]{1,0:T(8,128)S(1)} %shard_map.77.refs_0_), channel_id=1, source_target_pairs={{0,4},{1,5},{2,6},{3,7},{4,0},{5,1},{6,2},{7,3},{8,12},{9,13},{10,... | collective-permute-start | bytes 2457608 | tf_op jit(solution)/shard_map/ppermute | solution.py:404
  30.3 7.1 %collective-permute-done.15.refs_8_.refs_2_ = f32[160,640]{1,0:T(8,128)S(1)} collective-permute-done((f32[160,640]{1,0:T(8,128)S(1)}, f32[160,640]{1,0:T(8,128)S(1)}, u32[]{:S(2)}, u32[]{:S(2)}) %collective-permute-start.15) | collective-permute-done | bytes 409632 | tf_op jit(solution)/shard_map/ppermute | solution.py:404
  38.7 14.0 %collective-permute-start.13 = (f32[160,640]{1,0:T(8,128)S(1)}, f32[160,640]{1,0:T(8,128)S(1)}, u32[]{:S(2)}, u32[]{:S(2)}) collective-permute-start(f32[160,640]{1,0:T(8,128)S(1)} %collective-permute-done.11.refs_4_), channel_id=1, source_target_pairs={{0,1},{1,0},{2,3},{3,2},{4,5},{5,4},{6,7},{7,6},{8,9},{9,8},{10,11... | collective-permute-start | bytes 1228808 | tf_op jit(solution)/shard_map/ppermute | solution.py:404
  52.7 16.7 %collective-permute-done.28.refs_1_ = f32[256,640]{1,0:T(8,128)S(1)} collective-permute-done((f32[256,640]{1,0:T(8,128)S(1)}, f32[256,640]{1,0:T(8,128)S(1)}, u32[]{:S(2)}, u32[]{:S(2)}) %collective-permute-start.28) | collective-permute-done | bytes 655392 | tf_op jit(solution)/shard_map/ppermute | solution.py:404
  70.9 3.0 %collective-permute-start.2 = (f32[160,640]{1,0:T(8,128)S(1)}, f32[160,640]{1,0:T(8,128)S(1)}, u32[]{:S(2)}, u32[]{:S(2)}) collective-permute-start(f32[160,640]{1,0:T(8,128)S(1)} %shard_map.73.refs_0_), channel_id=1, source_target_pairs={{0,16},{1,17},{2,18},{3,19},{4,20},{5,21},{6,22},{7,23},{8,24},{9,... | collective-permute-start | bytes 1228808 | tf_op jit(solution)/shard_map/ppermute | solution.py:404
  76.9 9.0 %shard_map.79 = (f32[256,640]{1,0:T(8,128)S(1)}, f32[256,640]{1,0:T(8,128)S(1)}, f32[128,640]{1,0:T(8,128)S(1)}, f32[256,640]{1,0:T(8,128)S(1)}, f32[256,640]{1,0:T(8,128)S(1)}, /*index=5*/f32[128,640]{1,0:T(8,128)S(1)}) custom-call(s32[23]{0:T(128)S(1)} %stack.63.s_ref, f32[640,640]{1,0:T(8,128)S(1)} %shard_map.78.refs_0_, ...), custom_call_target="tpu_custom_call" | custom-call | flops 6291456000 | bytes 13107200 | tf_op jit(solution)/shard_map/pallas_call | solution.py:142
  85.9 13.8 %collective-permute-done.2.refs_2_ = f32[160,640]{1,0:T(8,128)S(1)} collective-permute-done((f32[160,640]{1,0:T(8,128)S(1)}, f32[160,640]{1,0:T(8,128)S(1)}, u32[]{:S(2)}, u32[]{:S(2)}) %collective-permute-start.2) | collective-permute-done | bytes 409632 | tf_op jit(solution)/shard_map/ppermute | solution.py:404
  101.6 3.5 %collective-permute-start.23 = (f32[256,640]{1,0:T(8,128)S(1)}, f32[256,640]{1,0:T(8,128)S(1)}, u32[]{:S(2)}, u32[]{:S(2)}) collective-permute-start(f32[256,640]{1,0:T(8,128)S(1)} %get-tuple-element.33), channel_id=1, source_target_pairs={{4,5},{5,6},{6,7},{8,1},{9,2},{10,3},{12,13},{13,14},{14,15},{16,9... | collective-permute-start | bytes 1966088 | tf_op jit(solution)/shard_map/ppermute | solution.py:404
  105.2 5.6 %collective-permute-start.19 = (f32[256,640]{1,0:T(8,128)S(1)}, f32[256,640]{1,0:T(8,128)S(1)}, u32[]{:S(2)}, u32[]{:S(2)}) collective-permute-start(f32[256,640]{1,0:T(8,128)S(1)} %get-tuple-element.30.a), channel_id=1, source_target_pairs={{4,12},{5,13},{6,14},{7,15},{12,20},{13,21},{14,22},{15,23},{20,28... | collective-permute-start | bytes 1966088 | tf_op jit(solution)/shard_map/ppermute | solution.py:404
  110.8 2.2 %collective-permute-start.20 = (f32[256,640]{1,0:T(8,128)S(1)}, f32[256,640]{1,0:T(8,128)S(1)}, u32[]{:S(2)}, u32[]{:S(2)}) collective-permute-start(f32[256,640]{1,0:T(8,128)S(1)} %get-tuple-element.31), channel_id=1, source_target_pairs={{4,5},{5,6},{6,7},{8,1},{9,2},{10,3},{12,13},{13,14},{14,15},{16,9... | collective-permute-start | bytes 1966088 | tf_op jit(solution)/shard_map/ppermute | solution.py:404
  113.0 2.2 %collective-permute-start.33 = (f32[384,640]{1,0:T(8,128)S(1)}, f32[384,640]{1,0:T(8,128)S(1)}, u32[]{:S(2)}, u32[]{:S(2)}) collective-permute-start(f32[384,640]{1,0:T(8,128)S(1)} %collective-permute-done.30.refs_1_), channel_id=1, source_target_pairs={{1,8},{2,9},{3,10},{5,4},{6,5},{7,6},{9,16},{10,17},{11,18},{13,12... | collective-permute-start | bytes 2949128 | tf_op jit(solution)/shard_map/ppermute | solution.py:404
  117.4 4.3 %collective-permute-start.31 = (f32[384,640]{1,0:T(8,128)S(1)}, f32[384,640]{1,0:T(8,128)S(1)}, u32[]{:S(2)}, u32[]{:S(2)}) collective-permute-start(f32[384,640]{1,0:T(8,128)S(1)} %shard_map.84), channel_id=1, source_target_pairs={{0,1},{1,2},{2,3},{8,9},{9,10},{10,11},{12,5},{13,6},{14,7},{16,17... | collective-permute-start | bytes 2949128 | tf_op jit(solution)/shard_map/ppermute | solution.py:404
  121.7 4.1 %collective-permute-start.25 = (f32[128,640]{1,0:T(8,128)S(1)}, f32[128,640]{1,0:T(8,128)S(1)}, u32[]{:S(2)}, u32[]{:S(2)}) collective-permute-start(f32[128,640]{1,0:T(8,128)S(1)} %get-tuple-element.34.a), channel_id=1, source_target_pairs={{4,12},{5,13},{6,14},{7,15},{12,20},{13,21},{14,22},{15,23},{20,28... | collective-permute-start | bytes 983048 | tf_op jit(solution)/shard_map/ppermute | solution.py:404
  125.8 5.6 %collective-permute-done.19.b = f32[256,640]{1,0:T(8,128)S(1)} collective-permute-done((f32[256,640]{1,0:T(8,128)S(1)}, f32[256,640]{1,0:T(8,128)S(1)}, u32[]{:S(2)}, u32[]{:S(2)}) %collective-permute-start.19) | collective-permute-done | bytes 655392 | tf_op jit(solution)/shard_map/ppermute | solution.py:404
  131.4 5.3 %collective-permute-start.26 = (f32[128,640]{1,0:T(8,128)S(1)}, f32[128,640]{1,0:T(8,128)S(1)}, u32[]{:S(2)}, u32[]{:S(2)}) collective-permute-start(f32[128,640]{1,0:T(8,128)S(1)} %get-tuple-element.35), channel_id=1, source_target_pairs={{4,5},{5,6},{6,7},{8,1},{9,2},{10,3},{12,13},{13,14},{14,15},{16,9... | collective-permute-start | bytes 983048 | tf_op jit(solution)/shard_map/ppermute | solution.py:404
  140.4 4.8 %shard_map.75 = (f32[640,640]{1,0:T(8,128)S(1)}, f32[640,640]{1,0:T(8,128)S(1)}) custom-call(s32[23]{0:T(128)S(1)} %stack.63.s_ref, f32[160,640]{1,0:T(8,128)S(1)} %bitcast.25, f32[160,640]{1,0:T(8,128)S(1)} %collective-permute-done.4.refs_1_, f32[160,640]{1,0:T(8,128)S(1)} %collective-permute-done.5.refs_2_, f32[160,640]{1,0:T(8,128)S(1)} %collective-permute-done.6.refs_3_, ...), custom_call_target="tpu_custom_call" | custom-call | flops 3145728000 | bytes 11468800 | tf_op jit(solution)/shard_map/pallas_call | solution.py:142
  147.0 4.9 %shard_map.76 = (f32[640,640]{1,0:T(8,128)S(1)}, f32[640,640]{1,0:T(8,128)S(1)}) custom-call(s32[23]{0:T(128)S(1)} %stack.63.s_ref, f32[160,640]{1,0:T(8,128)S(1)} %shard_map.73.refs_0_, f32[160,640]{1,0:T(8,128)S(1)} %collective-permute-done.1.refs_1_, f32[160,640]{1,0:T(8,128)S(1)} %collective-permute-done.2.refs_2_, ...), custom_call_target="tpu_custom_call" | custom-call | flops 3145728000 | bytes 14745600 | tf_op jit(solution)/shard_map/pallas_call | solution.py:142
  152.1 4.9 %shard_map.85.refs_6_ = f32[640,640]{1,0:T(8,128)S(1)} custom-call(s32[23]{0:T(128)S(1)} %stack.63.s_ref, f32[640,640]{1,0:T(8,128)S(1)} %shard_map.78.refs_0_, f32[256,640]{1,0:T(8,128)S(1)} %collective-permute-done.32.refs_1_, f32[384,640]{1,0:T(8,128)S(1)} %collective-permute-done.33.refs_2_, f32[160,640]{1,0:T(8,128)S(1)} %bitcast.30, ...), custom_call_target="tpu_custom_call" | custom-call | flops 3145728000 | bytes 8192000 | tf_op jit(solution)/shard_map/pallas_call | solution.py:142
  157.6 4.2 %shard_map.86.refs_4_ = f32[2,640,640]{2,1,0:T(8,128)} custom-call(s32[23]{0:T(128)S(1)} %stack.63.s_ref, f32[256,640]{1,0:T(8,128)S(1)} %collective-permute-done.29.refs_0_, f32[384,640]{1,0:T(8,128)S(1)} %collective-permute-done.31.refs_1_, f32[160,640]{1,0:T(8,128)S(1)} %collective-permute-done.15.refs_8_.refs_2_, ...), custom_call_target="tpu_custom_call" | custom-call | flops 1572864000 | bytes 8192000 | tf_op jit(solution)/shard_map/pallas_call | solution.py:142
  161.7 21.5 %collective-permute-done.27.refs_3_ = f32[128,640]{1,0:T(8,128)S(1)} collective-permute-done((f32[128,640]{1,0:T(8,128)S(1)}, f32[128,640]{1,0:T(8,128)S(1)}, u32[]{:S(2)}, u32[]{:S(2)}) %collective-permute-start.27) | collective-permute-done | bytes 327712 | tf_op jit(solution)/shard_map/ppermute | solution.py:404
  (70 shorter events, 29.5 us)
Async XLA Ops:
  2.6 21.0 %collective-permute-start.4 = (f32[160,640]{1,0:T(8,128)}, f32[160,640]{1,0:T(8,128)S(1)}, u32[]{:S(2)}, u32[]{:S(2)}) collective-permute-start(f32[160,640]{1,0:T(8,128)} %bitcast.23), channel_id=1, source_target_pairs={{0,2},{1,3},{2,0},{3,1},{4,6},{5,7},{6,4},{7,5},{8,10},{9,11},{10,... | collective-permute-start | bytes 1228808 | tf_op jit(solution)/shard_map/ppermute | solution.py:404
  8.9 66.0 %collective-permute-start.14 = (f32[640,640]{1,0:T(8,128)S(1)}, f32[640,640]{1,0:T(8,128)S(1)}, u32[]{:S(2)}, u32[]{:S(2)}) collective-permute-start(f32[640,640]{1,0:T(8,128)S(1)} %get-tuple-element.29), channel_id=1, source_target_pairs={{1,0},{2,1},{3,2},{5,4},{6,5},{7,6},{9,8},{10,9},{11,10},{13,12},{... | collective-permute-start | bytes 4915208 | tf_op jit(solution)/shard_map/ppermute | solution.py:404
  12.7 14.5 %collective-permute-start.5 = (f32[160,640]{1,0:T(8,128)S(1)}, f32[160,640]{1,0:T(8,128)S(1)}, u32[]{:S(2)}, u32[]{:S(2)}) collective-permute-start(f32[160,640]{1,0:T(8,128)S(1)} %bitcast.24), channel_id=1, source_target_pairs={{0,1},{1,0},{2,3},{3,2},{4,5},{5,4},{6,7},{7,6},{8,9},{9,8},{10,11... | collective-permute-start | bytes 1228808 | tf_op jit(solution)/shard_map/ppermute | solution.py:404
  12.8 16.7 %collective-permute-start.11 = (f32[160,640]{1,0:T(8,128)S(1)}, f32[160,640]{1,0:T(8,128)S(1)}, u32[]{:S(2)}, u32[]{:S(2)}) collective-permute-start(f32[160,640]{1,0:T(8,128)S(1)} %bitcast.26), channel_id=1, source_target_pairs={{0,2},{1,3},{2,0},{3,1},{4,6},{5,7},{6,4},{7,5},{8,10},{9,11},{10,... | collective-permute-start | bytes 1228808 | tf_op jit(solution)/shard_map/ppermute | solution.py:404
  27.3 42.6 %collective-permute-start.10 = (f32[320,640]{1,0:T(8,128)S(1)}, f32[320,640]{1,0:T(8,128)S(1)}, u32[]{:S(2)}, u32[]{:S(2)}) collective-permute-start(f32[320,640]{1,0:T(8,128)S(1)} %shard_map.77.refs_0_), channel_id=1, source_target_pairs={{0,4},{1,5},{2,6},{3,7},{4,0},{5,1},{6,2},{7,3},{8,12},{9,13},{10,... | collective-permute-start | bytes 2457608 | tf_op jit(solution)/shard_map/ppermute | solution.py:404
  29.5 39.9 %collective-permute-start.28 = (f32[256,640]{1,0:T(8,128)S(1)}, f32[256,640]{1,0:T(8,128)S(1)}, u32[]{:S(2)}, u32[]{:S(2)}) collective-permute-start(f32[256,640]{1,0:T(8,128)S(1)} %get-tuple-element.36), channel_id=1, source_target_pairs={{0,4},{1,5},{2,6},{3,7},{4,0},{5,1},{6,2},{7,3},{8,12},{9,13},{10,... | collective-permute-start | bytes 1966088 | tf_op jit(solution)/shard_map/ppermute | solution.py:404
  37.4 32.4 %collective-permute-start.16 = (f32[160,640]{1,0:T(8,128)S(1)}, f32[160,640]{1,0:T(8,128)S(1)}, u32[]{:S(2)}, u32[]{:S(2)}) collective-permute-start(f32[160,640]{1,0:T(8,128)S(1)} %collective-permute-done.15.refs_8_.refs_2_), channel_id=1, source_target_pairs={{0,2},{1,3},{2,0},{3,1},{4,6},{5,7},{6,4},{7,5},{8,10},{9,11},{10,... | collective-permute-start | bytes 1228808 | tf_op jit(solution)/shard_map/ppermute | solution.py:404
  38.7 32.2 %collective-permute-start.13 = (f32[160,640]{1,0:T(8,128)S(1)}, f32[160,640]{1,0:T(8,128)S(1)}, u32[]{:S(2)}, u32[]{:S(2)}) collective-permute-start(f32[160,640]{1,0:T(8,128)S(1)} %collective-permute-done.11.refs_4_), channel_id=1, source_target_pairs={{0,1},{1,0},{2,3},{3,2},{4,5},{5,4},{6,7},{7,6},{8,9},{9,8},{10,11... | collective-permute-start | bytes 1228808 | tf_op jit(solution)/shard_map/ppermute | solution.py:404
  69.9 40.8 %collective-permute-start.30 = (f32[384,640]{1,0:T(8,128)S(1)}, f32[384,640]{1,0:T(8,128)S(1)}, u32[]{:S(2)}, u32[]{:S(2)}) collective-permute-start(f32[384,640]{1,0:T(8,128)S(1)} %get-tuple-element.37), channel_id=1, source_target_pairs={{0,4},{1,5},{2,6},{3,7},{4,0},{5,1},{6,2},{7,3},{8,12},{9,13},{10,... | collective-permute-start | bytes 2949128 | tf_op jit(solution)/shard_map/ppermute | solution.py:404
  70.9 28.8 %collective-permute-start.2 = (f32[160,640]{1,0:T(8,128)S(1)}, f32[160,640]{1,0:T(8,128)S(1)}, u32[]{:S(2)}, u32[]{:S(2)}) collective-permute-start(f32[160,640]{1,0:T(8,128)S(1)} %shard_map.73.refs_0_), channel_id=1, source_target_pairs={{0,16},{1,17},{2,18},{3,19},{4,20},{5,21},{6,22},{7,23},{8,24},{9,... | collective-permute-start | bytes 1228808 | tf_op jit(solution)/shard_map/ppermute | solution.py:404
  73.9 27.7 %collective-permute-start.3 = (f32[160,640]{1,0:T(8,128)S(1)}, f32[160,640]{1,0:T(8,128)S(1)}, u32[]{:S(2)}, u32[]{:S(2)}) collective-permute-start(f32[160,640]{1,0:T(8,128)S(1)} %shard_map.73.refs_0_), channel_id=1, source_target_pairs={{0,24},{1,25},{2,26},{3,27},{4,28},{5,29},{6,30},{7,31},{8,0},{9,1... | collective-permute-start | bytes 1228808 | tf_op jit(solution)/shard_map/ppermute | solution.py:404
  73.9 31.3 %collective-permute-start.6 = (f32[160,640]{1,0:T(8,128)S(1)}, f32[160,640]{1,0:T(8,128)S(1)}, u32[]{:S(2)}, u32[]{:S(2)}) collective-permute-start(f32[160,640]{1,0:T(8,128)S(1)} %collective-permute-done.4.refs_1_), channel_id=1, source_target_pairs={{0,1},{1,0},{2,3},{3,2},{4,5},{5,4},{6,7},{7,6},{8,9},{9,8},{10,11... | collective-permute-start | bytes 1228808 | tf_op jit(solution)/shard_map/ppermute | solution.py:404
  75.0 38.0 %collective-permute-start.32 = (f32[256,640]{1,0:T(8,128)S(1)}, f32[256,640]{1,0:T(8,128)S(1)}, u32[]{:S(2)}, u32[]{:S(2)}) collective-permute-start(f32[256,640]{1,0:T(8,128)S(1)} %collective-permute-done.28.refs_1_), channel_id=1, source_target_pairs={{1,8},{2,9},{3,10},{5,4},{6,5},{7,6},{9,16},{10,17},{11,18},{13,12... | collective-permute-start | bytes 1966088 | tf_op jit(solution)/shard_map/ppermute | solution.py:404
  99.7 17.7 %collective-permute-start.22 = (f32[256,640]{1,0:T(8,128)S(1)}, f32[256,640]{1,0:T(8,128)S(1)}, u32[]{:S(2)}, u32[]{:S(2)}) collective-permute-start(f32[256,640]{1,0:T(8,128)S(1)} %get-tuple-element.32.a), channel_id=1, source_target_pairs={{4,12},{5,13},{6,14},{7,15},{12,20},{13,21},{14,22},{15,23},{20,28... | collective-permute-start | bytes 1966088 | tf_op jit(solution)/shard_map/ppermute | solution.py:404
  101.6 20.1 %collective-permute-start.23 = (f32[256,640]{1,0:T(8,128)S(1)}, f32[256,640]{1,0:T(8,128)S(1)}, u32[]{:S(2)}, u32[]{:S(2)}) collective-permute-start(f32[256,640]{1,0:T(8,128)S(1)} %get-tuple-element.33), channel_id=1, source_target_pairs={{4,5},{5,6},{6,7},{8,1},{9,2},{10,3},{12,13},{13,14},{14,15},{16,9... | collective-permute-start | bytes 1966088 | tf_op jit(solution)/shard_map/ppermute | solution.py:404
  105.2 26.3 %collective-permute-start.19 = (f32[256,640]{1,0:T(8,128)S(1)}, f32[256,640]{1,0:T(8,128)S(1)}, u32[]{:S(2)}, u32[]{:S(2)}) collective-permute-start(f32[256,640]{1,0:T(8,128)S(1)} %get-tuple-element.30.a), channel_id=1, source_target_pairs={{4,12},{5,13},{6,14},{7,15},{12,20},{13,21},{14,22},{15,23},{20,28... | collective-permute-start | bytes 1966088 | tf_op jit(solution)/shard_map/ppermute | solution.py:404
  110.8 27.6 %collective-permute-start.20 = (f32[256,640]{1,0:T(8,128)S(1)}, f32[256,640]{1,0:T(8,128)S(1)}, u32[]{:S(2)}, u32[]{:S(2)}) collective-permute-start(f32[256,640]{1,0:T(8,128)S(1)} %get-tuple-element.31), channel_id=1, source_target_pairs={{4,5},{5,6},{6,7},{8,1},{9,2},{10,3},{12,13},{13,14},{14,15},{16,9... | collective-permute-start | bytes 1966088 | tf_op jit(solution)/shard_map/ppermute | solution.py:404
  113.0 39.0 %collective-permute-start.33 = (f32[384,640]{1,0:T(8,128)S(1)}, f32[384,640]{1,0:T(8,128)S(1)}, u32[]{:S(2)}, u32[]{:S(2)}) collective-permute-start(f32[384,640]{1,0:T(8,128)S(1)} %collective-permute-done.30.refs_1_), channel_id=1, source_target_pairs={{1,8},{2,9},{3,10},{5,4},{6,5},{7,6},{9,16},{10,17},{11,18},{13,12... | collective-permute-start | bytes 2949128 | tf_op jit(solution)/shard_map/ppermute | solution.py:404
  117.4 40.2 %collective-permute-start.31 = (f32[384,640]{1,0:T(8,128)S(1)}, f32[384,640]{1,0:T(8,128)S(1)}, u32[]{:S(2)}, u32[]{:S(2)}) collective-permute-start(f32[384,640]{1,0:T(8,128)S(1)} %shard_map.84), channel_id=1, source_target_pairs={{0,1},{1,2},{2,3},{8,9},{9,10},{10,11},{12,5},{13,6},{14,7},{16,17... | collective-permute-start | bytes 2949128 | tf_op jit(solution)/shard_map/ppermute | solution.py:404
  121.7 23.8 %collective-permute-start.25 = (f32[128,640]{1,0:T(8,128)S(1)}, f32[128,640]{1,0:T(8,128)S(1)}, u32[]{:S(2)}, u32[]{:S(2)}) collective-permute-start(f32[128,640]{1,0:T(8,128)S(1)} %get-tuple-element.34.a), channel_id=1, source_target_pairs={{4,12},{5,13},{6,14},{7,15},{12,20},{13,21},{14,22},{15,23},{20,28... | collective-permute-start | bytes 983048 | tf_op jit(solution)/shard_map/ppermute | solution.py:404
  138.3 19.2 %collective-permute-start.29 = (f32[256,640]{1,0:T(8,128)S(1)}, f32[256,640]{1,0:T(8,128)S(1)}, u32[]{:S(2)}, u32[]{:S(2)}) collective-permute-start(f32[256,640]{1,0:T(8,128)S(1)} %shard_map.83), channel_id=1, source_target_pairs={{0,1},{1,2},{2,3},{8,9},{9,10},{10,11},{12,5},{13,6},{14,7},{16,17... | collective-permute-start | bytes 1966088 | tf_op jit(solution)/shard_map/ppermute | solution.py:404
  145.5 37.7 %collective-permute-start.24 = (f32[256,640]{1,0:T(8,128)S(1)}, f32[256,640]{1,0:T(8,128)S(1)}, u32[]{:S(2)}, u32[]{:S(2)}) collective-permute-start(f32[256,640]{1,0:T(8,128)S(1)} %shard_map.81), channel_id=1, source_target_pairs={{0,4},{1,5},{2,6},{3,7},{4,0},{5,1},{6,2},{7,3},{8,12},{9,13},{10,... | collective-permute-start | bytes 1966088 | tf_op jit(solution)/shard_map/ppermute | solution.py:404
  145.6 37.7 %collective-permute-start.21 = (f32[256,640]{1,0:T(8,128)S(1)}, f32[256,640]{1,0:T(8,128)S(1)}, u32[]{:S(2)}, u32[]{:S(2)}) collective-permute-start(f32[256,640]{1,0:T(8,128)S(1)} %shard_map.80), channel_id=1, source_target_pairs={{0,4},{1,5},{2,6},{3,7},{4,0},{5,1},{6,2},{7,3},{8,12},{9,13},{10,... | collective-permute-start | bytes 1966088 | tf_op jit(solution)/shard_map/ppermute | solution.py:404
  152.0 31.2 %collective-permute-start.27 = (f32[128,640]{1,0:T(8,128)S(1)}, f32[128,640]{1,0:T(8,128)S(1)}, u32[]{:S(2)}, u32[]{:S(2)}) collective-permute-start(f32[128,640]{1,0:T(8,128)S(1)} %shard_map.82), channel_id=1, source_target_pairs={{0,4},{1,5},{2,6},{3,7},{4,0},{5,1},{6,2},{7,3},{8,12},{9,13},{10,... | collective-permute-start | bytes 983048 | tf_op jit(solution)/shard_map/ppermute | solution.py:404
  (15 other events, 139.8 us)

commit v2 on v1

--- a/solution.py
+++ b/solution.py
@@ -366,26 +366,31 @@
     )(mine[None], hop, hop_far, back_far)
 
 
-def finish(partial, scal, other_sum, returned):
-    ops = Operands()
-    buffers = [ops.stacked(other_sum), ops.stacked(*returned)]
-    place = ops.add(partial)
-
-    def kernel(get, put, pass_on, s_ref):
-        total = get(0)
-        put(0, masked(total + get(1), s_ref))
-
-    return fetched(
-        kernel,
-        ops.inputs,
-        buffers,
-        [sds(partial.shape)],
-        [(other_sum.shape, [0])],
-        scalars=scal,
-        root=lambda s_ref: 1 - s_ref[0],
-        aliases={1 + place: 0},
-        mib=12,
-    )[0]
+def finish(partial, scal, other_sum, returned, first):
+    _, _, width = partial.shape
+    rows = sum(x.shape[0] for x in returned)
+    n = len(returned)
+
+    def kernel(s_ref, _, other_ref, *refs):
+        at = 0
+        for piece in refs[:n]:
+            span = pl.ds(at, piece.shape[0])
+            row = lax.broadcasted_iota(jnp.int32, piece.shape, 0) + first + at
+            col = lax.broadcasted_iota(jnp.int32, piece.shape, 1)
+            total = other_ref[span, :] + piece[...]
+            refs[n][0, span, :] = jnp.where((row < s_ref[1]) & (col < s_ref[2]), total, 0.0)
+            at += piece.shape[0]
+
+    return call(
+        kernel,
+        sds(partial.shape),
+        scalars=1,
+        in_specs=[pl.BlockSpec(memory_space=pl.ANY), pl.BlockSpec((rows, width), lambda *_: (first // rows, 0))]
+        + [whole(x.shape) for x in returned],
+        out_specs=pl.BlockSpec((1, rows, width), lambda s, s_ref: (1 - s_ref[0], first // rows, 0)),
+        nbytes=12 * rows * width,
+        aliases={1: 0},
+    )(scal, partial, other_sum, *returned)
 
 
 def on_device(n_l, n_r, states, left_env, right_env, left_op, right_op, sizes_left, sizes_right):
@@ -458,7 +463,8 @@
     own_sum, other_sum = right_local(scal, at_e, all_e, rows_r, own_split, other_split, sums)
     own_sum = own_hop(scal, at_l, twin_hop, op_r, all_lo, own_sum)
     partial = own_back(scal, at_l, states.shape, twin_mid, all_n, own_sum)
-    return finish(partial, scal, other_sum, returned)
+    partial = finish(partial, scal, other_sum, returned[:-1], 0)
+    return finish(partial, scal, other_sum, returned[-1:], cap - pieces[-1])
 
 
 def solution(mesh):

time: 186 us -> 185 us (level)
  waiting for transfers between devices: 70.7 us -> 67.7 us
    pallas_call x0 -> x2, Pallas kernels: none -> 3.05 us  [finish(): call(kernel, sds(partial.shape), scalars=1, in_specs=[pl.BlockSpec(memory...]
    ppermute x34, waiting for transfers between devices: 70.7 us -> 67.7 us  [move(): return lax.ppermute(value, AXES, pairs)]
    pallas_call x11 -> x10, Pallas kernels: 34.9 us -> 33 us  [fetched(): call(body, tuple(outs), scalars=1, in_specs=in_specs, out_specs=out_specs...]
  transfers between devices with their start and end apart: 34 -> 34, of which waited for: 9 -> 12; matrix products, arithmetic and copies ran while one was open for 0% -> 0% of each run, Pallas kernels for 19% -> 20%
where the time goes in v2:
time: 185 us; the launch traced here: 184 us
  starting transfers between devices  74.8 us (40%)
  waiting for transfers between devices  67.7 us (37%)
  Pallas kernels  38.1 us (21%)
  local copies, waits for them, and re-layouts  2.04 us (1%)
    ppermute x34, starting transfers between devices, move(): return lax.ppermute(value, AXES, pairs)  74.8 us
    ppermute x34, waiting for transfers between devices, move(): return lax.ppermute(value, AXES, pairs)  67.7 us
    pallas_call x10, Pallas kernels, fetched(): call(body, tuple(outs), scalars=1, in_specs=in_specs, out_specs=out_specs...  33 us
  transfers between devices with their start and end apart: 34, of which 12 were waited for; matrix products, arithmetic and copies ran while one was open for 0% of the time, Pallas kernels for 20%

profile of v2, /device:TPU:11, one launch (start us, length us, event | category | flops | bytes accessed | tf_op | source)
XLA Modules:
  0.0 184.4 jit_solution(4496748465774087587)
XLA Ops:
  3.8 2.2 %collective-permute-start.8 = (f32[160,640]{1,0:T(8,128)}, f32[160,640]{1,0:T(8,128)S(1)}, u32[]{:S(2)}, u32[]{:S(2)}) collective-permute-start(f32[160,640]{1,0:T(8,128)} %bitcast.26), channel_id=1, source_target_pairs={{4,0},{5,1},{6,2},{7,3},{8,4},{9,5},{10,6},{11,7},{12,8},{13,9},{1... | collective-permute-start | bytes 1228808 | tf_op jit(solution)/shard_map/ppermute | solution.py:409
  11.2 3.7 %collective-permute-start.24 = (f32[640,640]{1,0:T(8,128)S(1)}, f32[640,640]{1,0:T(8,128)S(1)}, u32[]{:S(2)}, u32[]{:S(2)}) collective-permute-start(f32[640,640]{1,0:T(8,128)S(1)} %get-tuple-element.32), channel_id=1, source_target_pairs={{1,0},{2,1},{3,2},{5,4},{6,5},{7,6},{9,8},{10,9},{11,10},{13,12},{... | collective-permute-start | bytes 4915208 | tf_op jit(solution)/shard_map/ppermute | solution.py:409
  16.3 2.2 %collective-permute-done.1.refs_2_ = f32[80,640]{1,0:T(8,128)S(1)} collective-permute-done((f32[80,640]{1,0:T(8,128)}, f32[80,640]{1,0:T(8,128)S(1)}, u32[]{:S(2)}, u32[]{:S(2)}) %collective-permute-start.1) | collective-permute-done | bytes 204832 | tf_op jit(solution)/shard_map/ppermute | solution.py:409
  21.6 12.9 %collective-permute-done.17.refs_1_ = f32[80,640]{1,0:T(8,128)S(1)} collective-permute-done((f32[80,640]{1,0:T(8,128)S(1)}, f32[80,640]{1,0:T(8,128)S(1)}, u32[]{:S(2)}, u32[]{:S(2)}) %collective-permute-start.17) | collective-permute-done | bytes 204832 | tf_op jit(solution)/shard_map/ppermute | solution.py:409
  39.2 6.8 %collective-permute-done.21.refs_1_ = f32[160,640]{1,0:T(8,128)S(1)} collective-permute-done((f32[160,640]{1,0:T(8,128)S(1)}, f32[160,640]{1,0:T(8,128)S(1)}, u32[]{:S(2)}, u32[]{:S(2)}) %collective-permute-start.21) | collective-permute-done | bytes 409632 | tf_op jit(solution)/shard_map/ppermute | solution.py:409
  46.2 6.8 %collective-permute-done.18.refs_1_ = f32[160,640]{1,0:T(8,128)S(1)} collective-permute-done((f32[160,640]{1,0:T(8,128)S(1)}, f32[160,640]{1,0:T(8,128)S(1)}, u32[]{:S(2)}, u32[]{:S(2)}) %collective-permute-start.18) | collective-permute-done | bytes 409632 | tf_op jit(solution)/shard_map/ppermute | solution.py:409
  53.0 12.0 %collective-permute-start.10 = (f32[160,640]{1,0:T(8,128)S(1)}, f32[160,640]{1,0:T(8,128)S(1)}, u32[]{:S(2)}, u32[]{:S(2)}) collective-permute-start(f32[160,640]{1,0:T(8,128)S(1)} %collective-permute-done.8.refs_2_.refs_8_), channel_id=1, source_target_pairs={{0,1},{1,0},{2,3},{3,2},{4,5},{5,4},{6,7},{7,6},{8,9},{9,8},{10,11... | collective-permute-start | bytes 1228808 | tf_op jit(solution)/shard_map/ppermute | solution.py:409
  65.1 6.8 %collective-permute-start.16 = (f32[160,640]{1,0:T(8,128)S(1)}, f32[160,640]{1,0:T(8,128)S(1)}, u32[]{:S(2)}, u32[]{:S(2)}) collective-permute-start(f32[160,640]{1,0:T(8,128)S(1)} %collective-permute-done.14.refs_4_), channel_id=1, source_target_pairs={{0,1},{1,0},{2,3},{3,2},{4,5},{5,4},{6,7},{7,6},{8,9},{9,8},{10,11... | collective-permute-start | bytes 1228808 | tf_op jit(solution)/shard_map/ppermute | solution.py:409
  80.0 9.0 %shard_map.83 = (f32[256,640]{1,0:T(8,128)S(1)}, f32[256,640]{1,0:T(8,128)S(1)}, f32[128,640]{1,0:T(8,128)S(1)}, f32[256,640]{1,0:T(8,128)S(1)}, f32[256,640]{1,0:T(8,128)S(1)}, /*index=5*/f32[128,640]{1,0:T(8,128)S(1)}) custom-call(s32[23]{0:T(128)S(1)} %stack.63.s_ref, f32[640,640]{1,0:T(8,128)S(1)} %shard_map.74.refs_0_, ...), custom_call_target="tpu_custom_call" | custom-call | flops 6291456000 | bytes 13107200 | tf_op jit(solution)/shard_map/pallas_call | solution.py:142
  89.0 11.4 %collective-permute-done.19.refs_2_ = f32[160,640]{1,0:T(8,128)S(1)} collective-permute-done((f32[160,640]{1,0:T(8,128)S(1)}, f32[160,640]{1,0:T(8,128)S(1)}, u32[]{:S(2)}, u32[]{:S(2)}) %collective-permute-start.19) | collective-permute-done | bytes 409632 | tf_op jit(solution)/shard_map/ppermute | solution.py:409
  105.0 5.6 %collective-permute-start.25 = (f32[256,640]{1,0:T(8,128)S(1)}, f32[256,640]{1,0:T(8,128)S(1)}, u32[]{:S(2)}, u32[]{:S(2)}) collective-permute-start(f32[256,640]{1,0:T(8,128)S(1)} %get-tuple-element.33.a), channel_id=1, source_target_pairs={{4,12},{5,13},{6,14},{7,15},{12,20},{13,21},{14,22},{15,23},{20,28... | collective-permute-start | bytes 1966088 | tf_op jit(solution)/shard_map/ppermute | solution.py:409
  110.6 2.2 %collective-permute-start.26 = (f32[256,640]{1,0:T(8,128)S(1)}, f32[256,640]{1,0:T(8,128)S(1)}, u32[]{:S(2)}, u32[]{:S(2)}) collective-permute-start(f32[256,640]{1,0:T(8,128)S(1)} %get-tuple-element.34), channel_id=1, source_target_pairs={{4,5},{5,6},{6,7},{8,1},{9,2},{10,3},{12,13},{13,14},{14,15},{16,9... | collective-permute-start | bytes 1966088 | tf_op jit(solution)/shard_map/ppermute | solution.py:409
  112.8 2.2 %collective-permute-start.13 = (f32[384,640]{1,0:T(8,128)S(1)}, f32[384,640]{1,0:T(8,128)S(1)}, u32[]{:S(2)}, u32[]{:S(2)}) collective-permute-start(f32[384,640]{1,0:T(8,128)S(1)} %collective-permute-done.6.refs_1_), channel_id=1, source_target_pairs={{1,8},{2,9},{3,10},{5,4},{6,5},{7,6},{9,16},{10,17},{11,18},{13,12... | collective-permute-start | bytes 2949128 | tf_op jit(solution)/shard_map/ppermute | solution.py:409
  117.0 4.5 %collective-permute-start.7 = (f32[384,640]{1,0:T(8,128)S(1)}, f32[384,640]{1,0:T(8,128)S(1)}, u32[]{:S(2)}, u32[]{:S(2)}) collective-permute-start(f32[384,640]{1,0:T(8,128)S(1)} %shard_map.77), channel_id=1, source_target_pairs={{0,1},{1,2},{2,3},{8,9},{9,10},{10,11},{12,5},{13,6},{14,7},{16,17... | collective-permute-start | bytes 2949128 | tf_op jit(solution)/shard_map/ppermute | solution.py:409
  121.6 4.1 %collective-permute-start.31 = (f32[128,640]{1,0:T(8,128)S(1)}, f32[128,640]{1,0:T(8,128)S(1)}, u32[]{:S(2)}, u32[]{:S(2)}) collective-permute-start(f32[128,640]{1,0:T(8,128)S(1)} %get-tuple-element.37.a), channel_id=1, source_target_pairs={{4,12},{5,13},{6,14},{7,15},{12,20},{13,21},{14,22},{15,23},{20,28... | collective-permute-start | bytes 983048 | tf_op jit(solution)/shard_map/ppermute | solution.py:409
  125.7 5.4 %collective-permute-done.25.b = f32[256,640]{1,0:T(8,128)S(1)} collective-permute-done((f32[256,640]{1,0:T(8,128)S(1)}, f32[256,640]{1,0:T(8,128)S(1)}, u32[]{:S(2)}, u32[]{:S(2)}) %collective-permute-start.25) | collective-permute-done | bytes 655392 | tf_op jit(solution)/shard_map/ppermute | solution.py:409
  131.1 5.5 %collective-permute-start.32 = (f32[128,640]{1,0:T(8,128)S(1)}, f32[128,640]{1,0:T(8,128)S(1)}, u32[]{:S(2)}, u32[]{:S(2)}) collective-permute-start(f32[128,640]{1,0:T(8,128)S(1)} %get-tuple-element.38), channel_id=1, source_target_pairs={{4,5},{5,6},{6,7},{8,1},{9,2},{10,3},{12,13},{13,14},{14,15},{16,9... | collective-permute-start | bytes 983048 | tf_op jit(solution)/shard_map/ppermute | solution.py:409
  140.3 4.8 %shard_map.79 = (f32[640,640]{1,0:T(8,128)S(1)}, f32[640,640]{1,0:T(8,128)S(1)}) custom-call(s32[23]{0:T(128)S(1)} %stack.63.s_ref, f32[160,640]{1,0:T(8,128)S(1)} %bitcast.25, f32[160,640]{1,0:T(8,128)S(1)} %collective-permute-done.21.refs_1_, f32[160,640]{1,0:T(8,128)S(1)} %collective-permute-done.22.refs_2_, ...), custom_call_target="tpu_custom_call" | custom-call | flops 3145728000 | bytes 11468800 | tf_op jit(solution)/shard_map/pallas_call | solution.py:142
  146.9 4.9 %shard_map.80 = (f32[640,640]{1,0:T(8,128)S(1)}, f32[640,640]{1,0:T(8,128)S(1)}) custom-call(s32[23]{0:T(128)S(1)} %stack.63.s_ref, f32[160,640]{1,0:T(8,128)S(1)} %shard_map.78.refs_0_, f32[160,640]{1,0:T(8,128)S(1)} %collective-permute-done.18.refs_1_, f32[160,640]{1,0:T(8,128)S(1)} %collective-permute-done.19.refs_2_, ...), custom_call_target="tpu_custom_call" | custom-call | flops 3145728000 | bytes 14745600 | tf_op jit(solution)/shard_map/pallas_call | solution.py:142
  152.0 4.9 %shard_map.81.refs_6_ = f32[640,640]{1,0:T(8,128)S(1)} custom-call(s32[23]{0:T(128)S(1)} %stack.63.s_ref, f32[640,640]{1,0:T(8,128)S(1)} %shard_map.74.refs_0_, f32[256,640]{1,0:T(8,128)S(1)} %collective-permute-done.12.refs_1_, f32[384,640]{1,0:T(8,128)S(1)} %collective-permute-done.13.refs_2_, f32[160,640]{1,0:T(8,128)S(1)} %bitcast.30, ...), custom_call_target="tpu_custom_call" | custom-call | flops 3145728000 | bytes 8192000 | tf_op jit(solution)/shard_map/pallas_call | solution.py:142
  156.9 3.2 %collective-permute-done.5.refs_0_ = f32[256,640]{1,0:T(8,128)S(1)} collective-permute-done((f32[256,640]{1,0:T(8,128)S(1)}, f32[256,640]{1,0:T(8,128)S(1)}, u32[]{:S(2)}, u32[]{:S(2)}) %collective-permute-start.5) | collective-permute-done | bytes 655392 | tf_op jit(solution)/shard_map/ppermute | solution.py:409
  160.1 4.2 %shard_map.82._ = f32[2,640,640]{2,1,0:T(8,128)} custom-call(s32[23]{0:T(128)S(1)} %stack.63.s_ref, f32[256,640]{1,0:T(8,128)S(1)} %collective-permute-done.5.refs_0_, f32[384,640]{1,0:T(8,128)S(1)} %collective-permute-done.7.refs_1_, f32[160,640]{1,0:T(8,128)S(1)} %collective-permute-done.8.refs_2_.refs_8_, ...), custom_call_target="tpu_custom_call" | custom-call | flops 1572864000 | bytes 8192000 | tf_op jit(solution)/shard_map/pallas_call | solution.py:142
  164.3 11.8 %collective-permute-done.27.refs_0_ = f32[256,640]{1,0:T(8,128)S(1)} collective-permute-done((f32[256,640]{1,0:T(8,128)S(1)}, f32[256,640]{1,0:T(8,128)S(1)}, u32[]{:S(2)}, u32[]{:S(2)}) %collective-permute-start.27) | collective-permute-done | bytes 655392 | tf_op jit(solution)/shard_map/ppermute | solution.py:409
  177.8 5.3 %collective-permute-done.33.refs_0_ = f32[128,640]{1,0:T(8,128)S(1)} collective-permute-done((f32[128,640]{1,0:T(8,128)S(1)}, f32[128,640]{1,0:T(8,128)S(1)}, u32[]{:S(2)}, u32[]{:S(2)}) %collective-permute-start.33) | collective-permute-done | bytes 327712 | tf_op jit(solution)/shard_map/ppermute | solution.py:409
  (71 shorter events, 40.4 us)
Async XLA Ops:
  2.3 18.9 %collective-permute-start.2 = (f32[80,640]{1,0:T(8,128)}, f32[80,640]{1,0:T(8,128)S(1)}, u32[]{:S(2)}, u32[]{:S(2)}) collective-permute-start(f32[80,640]{1,0:T(8,128)} %bitcast.19), channel_id=1, source_target_pairs={{0,24},{1,25},{2,26},{3,27},{4,28},{5,29},{6,30},{7,31},{8,0},{9,1... | collective-permute-start | bytes 614408 | tf_op jit(solution)/shard_map/ppermute | solution.py:409
  3.8 31.9 %collective-permute-start.8 = (f32[160,640]{1,0:T(8,128)}, f32[160,640]{1,0:T(8,128)S(1)}, u32[]{:S(2)}, u32[]{:S(2)}) collective-permute-start(f32[160,640]{1,0:T(8,128)} %bitcast.26), channel_id=1, source_target_pairs={{4,0},{5,1},{6,2},{7,3},{8,4},{9,5},{10,6},{11,7},{12,8},{13,9},{1... | collective-permute-start | bytes 1228808 | tf_op jit(solution)/shard_map/ppermute | solution.py:409
  11.2 66.9 %collective-permute-start.24 = (f32[640,640]{1,0:T(8,128)S(1)}, f32[640,640]{1,0:T(8,128)S(1)}, u32[]{:S(2)}, u32[]{:S(2)}) collective-permute-start(f32[640,640]{1,0:T(8,128)S(1)} %get-tuple-element.32), channel_id=1, source_target_pairs={{1,0},{2,1},{3,2},{5,4},{6,5},{7,6},{9,8},{10,9},{11,10},{13,12},{... | collective-permute-start | bytes 4915208 | tf_op jit(solution)/shard_map/ppermute | solution.py:409
  14.9 22.1 %collective-permute-start.14 = (f32[160,640]{1,0:T(8,128)S(1)}, f32[160,640]{1,0:T(8,128)S(1)}, u32[]{:S(2)}, u32[]{:S(2)}) collective-permute-start(f32[160,640]{1,0:T(8,128)S(1)} %bitcast.27), channel_id=1, source_target_pairs={{0,2},{1,3},{2,0},{3,1},{4,6},{5,7},{6,4},{7,5},{8,10},{9,11},{10,... | collective-permute-start | bytes 1228808 | tf_op jit(solution)/shard_map/ppermute | solution.py:409
  18.5 18.6 %collective-permute-start.15 = (f32[160,640]{1,0:T(8,128)S(1)}, f32[160,640]{1,0:T(8,128)S(1)}, u32[]{:S(2)}, u32[]{:S(2)}) collective-permute-start(f32[160,640]{1,0:T(8,128)S(1)} %bitcast.28), channel_id=1, source_target_pairs={{0,1},{1,0},{2,3},{3,2},{4,5},{5,4},{6,7},{7,6},{8,9},{9,8},{10,11... | collective-permute-start | bytes 1228808 | tf_op jit(solution)/shard_map/ppermute | solution.py:409
  37.1 34.8 %collective-permute-start.3 = (f32[320,640]{1,0:T(8,128)S(1)}, f32[320,640]{1,0:T(8,128)S(1)}, u32[]{:S(2)}, u32[]{:S(2)}) collective-permute-start(f32[320,640]{1,0:T(8,128)S(1)} %shard_map.73.refs_0_), channel_id=1, source_target_pairs={{0,4},{1,5},{2,6},{3,7},{4,0},{5,1},{6,2},{7,3},{8,12},{9,13},{10,... | collective-permute-start | bytes 2457608 | tf_op jit(solution)/shard_map/ppermute | solution.py:409
  37.1 27.9 %collective-permute-start.4 = (f32[256,640]{1,0:T(8,128)S(1)}, f32[256,640]{1,0:T(8,128)S(1)}, u32[]{:S(2)}, u32[]{:S(2)}) collective-permute-start(f32[256,640]{1,0:T(8,128)S(1)} %get-tuple-element.22), channel_id=1, source_target_pairs={{0,4},{1,5},{2,6},{3,7},{4,0},{5,1},{6,2},{7,3},{8,12},{9,13},{10,... | collective-permute-start | bytes 1966088 | tf_op jit(solution)/shard_map/ppermute | solution.py:409
  45.9 25.9 %collective-permute-start.9 = (f32[160,640]{1,0:T(8,128)S(1)}, f32[160,640]{1,0:T(8,128)S(1)}, u32[]{:S(2)}, u32[]{:S(2)}) collective-permute-start(f32[160,640]{1,0:T(8,128)S(1)} %collective-permute-done.8.refs_2_.refs_8_), channel_id=1, source_target_pairs={{0,2},{1,3},{2,0},{3,1},{4,6},{5,7},{6,4},{7,5},{8,10},{9,11},{10,... | collective-permute-start | bytes 1228808 | tf_op jit(solution)/shard_map/ppermute | solution.py:409
  53.0 20.4 %collective-permute-start.10 = (f32[160,640]{1,0:T(8,128)S(1)}, f32[160,640]{1,0:T(8,128)S(1)}, u32[]{:S(2)}, u32[]{:S(2)}) collective-permute-start(f32[160,640]{1,0:T(8,128)S(1)} %collective-permute-done.8.refs_2_.refs_8_), channel_id=1, source_target_pairs={{0,1},{1,0},{2,3},{3,2},{4,5},{5,4},{6,7},{7,6},{8,9},{9,8},{10,11... | collective-permute-start | bytes 1228808 | tf_op jit(solution)/shard_map/ppermute | solution.py:409
  71.8 38.8 %collective-permute-start.6 = (f32[384,640]{1,0:T(8,128)S(1)}, f32[384,640]{1,0:T(8,128)S(1)}, u32[]{:S(2)}, u32[]{:S(2)}) collective-permute-start(f32[384,640]{1,0:T(8,128)S(1)} %get-tuple-element.23), channel_id=1, source_target_pairs={{0,4},{1,5},{2,6},{3,7},{4,0},{5,1},{6,2},{7,3},{8,12},{9,13},{10,... | collective-permute-start | bytes 2949128 | tf_op jit(solution)/shard_map/ppermute | solution.py:409
  73.4 27.0 %collective-permute-start.19 = (f32[160,640]{1,0:T(8,128)S(1)}, f32[160,640]{1,0:T(8,128)S(1)}, u32[]{:S(2)}, u32[]{:S(2)}) collective-permute-start(f32[160,640]{1,0:T(8,128)S(1)} %shard_map.78.refs_0_), channel_id=1, source_target_pairs={{0,16},{1,17},{2,18},{3,19},{4,20},{5,21},{6,22},{7,23},{8,24},{9,... | collective-permute-start | bytes 1228808 | tf_op jit(solution)/shard_map/ppermute | solution.py:409
  74.8 28.1 %collective-permute-start.20 = (f32[160,640]{1,0:T(8,128)S(1)}, f32[160,640]{1,0:T(8,128)S(1)}, u32[]{:S(2)}, u32[]{:S(2)}) collective-permute-start(f32[160,640]{1,0:T(8,128)S(1)} %shard_map.78.refs_0_), channel_id=1, source_target_pairs={{0,24},{1,25},{2,26},{3,27},{4,28},{5,29},{6,30},{7,31},{8,0},{9,1... | collective-permute-start | bytes 1228808 | tf_op jit(solution)/shard_map/ppermute | solution.py:409
  76.8 28.2 %collective-permute-start.23 = (f32[160,640]{1,0:T(8,128)S(1)}, f32[160,640]{1,0:T(8,128)S(1)}, u32[]{:S(2)}, u32[]{:S(2)}) collective-permute-start(f32[160,640]{1,0:T(8,128)S(1)} %collective-permute-done.21.refs_1_), channel_id=1, source_target_pairs={{0,1},{1,0},{2,3},{3,2},{4,5},{5,4},{6,7},{7,6},{8,9},{9,8},{10,11... | collective-permute-start | bytes 1228808 | tf_op jit(solution)/shard_map/ppermute | solution.py:409
  78.1 34.7 %collective-permute-start.12 = (f32[256,640]{1,0:T(8,128)S(1)}, f32[256,640]{1,0:T(8,128)S(1)}, u32[]{:S(2)}, u32[]{:S(2)}) collective-permute-start(f32[256,640]{1,0:T(8,128)S(1)} %collective-permute-done.4.refs_1_), channel_id=1, source_target_pairs={{1,8},{2,9},{3,10},{5,4},{6,5},{7,6},{9,16},{10,17},{11,18},{13,12... | collective-permute-start | bytes 1966088 | tf_op jit(solution)/shard_map/ppermute | solution.py:409
  102.9 18.6 %collective-permute-start.29 = (f32[256,640]{1,0:T(8,128)S(1)}, f32[256,640]{1,0:T(8,128)S(1)}, u32[]{:S(2)}, u32[]{:S(2)}) collective-permute-start(f32[256,640]{1,0:T(8,128)S(1)} %get-tuple-element.36), channel_id=1, source_target_pairs={{4,5},{5,6},{6,7},{8,1},{9,2},{10,3},{12,13},{13,14},{14,15},{16,9... | collective-permute-start | bytes 1966088 | tf_op jit(solution)/shard_map/ppermute | solution.py:409
  105.0 26.1 %collective-permute-start.25 = (f32[256,640]{1,0:T(8,128)S(1)}, f32[256,640]{1,0:T(8,128)S(1)}, u32[]{:S(2)}, u32[]{:S(2)}) collective-permute-start(f32[256,640]{1,0:T(8,128)S(1)} %get-tuple-element.33.a), channel_id=1, source_target_pairs={{4,12},{5,13},{6,14},{7,15},{12,20},{13,21},{14,22},{15,23},{20,28... | collective-permute-start | bytes 1966088 | tf_op jit(solution)/shard_map/ppermute | solution.py:409
  110.6 27.6 %collective-permute-start.26 = (f32[256,640]{1,0:T(8,128)S(1)}, f32[256,640]{1,0:T(8,128)S(1)}, u32[]{:S(2)}, u32[]{:S(2)}) collective-permute-start(f32[256,640]{1,0:T(8,128)S(1)} %get-tuple-element.34), channel_id=1, source_target_pairs={{4,5},{5,6},{6,7},{8,1},{9,2},{10,3},{12,13},{13,14},{14,15},{16,9... | collective-permute-start | bytes 1966088 | tf_op jit(solution)/shard_map/ppermute | solution.py:409
  112.8 39.0 %collective-permute-start.13 = (f32[384,640]{1,0:T(8,128)S(1)}, f32[384,640]{1,0:T(8,128)S(1)}, u32[]{:S(2)}, u32[]{:S(2)}) collective-permute-start(f32[384,640]{1,0:T(8,128)S(1)} %collective-permute-done.6.refs_1_), channel_id=1, source_target_pairs={{1,8},{2,9},{3,10},{5,4},{6,5},{7,6},{9,16},{10,17},{11,18},{13,12... | collective-permute-start | bytes 2949128 | tf_op jit(solution)/shard_map/ppermute | solution.py:409
  117.0 43.0 %collective-permute-start.7 = (f32[384,640]{1,0:T(8,128)S(1)}, f32[384,640]{1,0:T(8,128)S(1)}, u32[]{:S(2)}, u32[]{:S(2)}) collective-permute-start(f32[384,640]{1,0:T(8,128)S(1)} %shard_map.77), channel_id=1, source_target_pairs={{0,1},{1,2},{2,3},{8,9},{9,10},{10,11},{12,5},{13,6},{14,7},{16,17... | collective-permute-start | bytes 2949128 | tf_op jit(solution)/shard_map/ppermute | solution.py:409
  121.6 23.8 %collective-permute-start.31 = (f32[128,640]{1,0:T(8,128)S(1)}, f32[128,640]{1,0:T(8,128)S(1)}, u32[]{:S(2)}, u32[]{:S(2)}) collective-permute-start(f32[128,640]{1,0:T(8,128)S(1)} %get-tuple-element.37.a), channel_id=1, source_target_pairs={{4,12},{5,13},{6,14},{7,15},{12,20},{13,21},{14,22},{15,23},{20,28... | collective-permute-start | bytes 983048 | tf_op jit(solution)/shard_map/ppermute | solution.py:409
  138.2 21.9 %collective-permute-start.5 = (f32[256,640]{1,0:T(8,128)S(1)}, f32[256,640]{1,0:T(8,128)S(1)}, u32[]{:S(2)}, u32[]{:S(2)}) collective-permute-start(f32[256,640]{1,0:T(8,128)S(1)} %shard_map.76), channel_id=1, source_target_pairs={{0,1},{1,2},{2,3},{8,9},{9,10},{10,11},{12,5},{13,6},{14,7},{16,17... | collective-permute-start | bytes 1966088 | tf_op jit(solution)/shard_map/ppermute | solution.py:409
  145.3 18.9 %collective-permute-start.30 = (f32[256,640]{1,0:T(8,128)S(1)}, f32[256,640]{1,0:T(8,128)S(1)}, u32[]{:S(2)}, u32[]{:S(2)}) collective-permute-start(f32[256,640]{1,0:T(8,128)S(1)} %shard_map.85), channel_id=1, source_target_pairs={{0,4},{1,5},{2,6},{3,7},{4,0},{5,1},{6,2},{7,3},{8,12},{9,13},{10,... | collective-permute-start | bytes 1966088 | tf_op jit(solution)/shard_map/ppermute | solution.py:409
  145.4 30.6 %collective-permute-start.27 = (f32[256,640]{1,0:T(8,128)S(1)}, f32[256,640]{1,0:T(8,128)S(1)}, u32[]{:S(2)}, u32[]{:S(2)}) collective-permute-start(f32[256,640]{1,0:T(8,128)S(1)} %shard_map.84), channel_id=1, source_target_pairs={{0,4},{1,5},{2,6},{3,7},{4,0},{5,1},{6,2},{7,3},{8,12},{9,13},{10,... | collective-permute-start | bytes 1966088 | tf_op jit(solution)/shard_map/ppermute | solution.py:409
  151.9 31.2 %collective-permute-start.33 = (f32[128,640]{1,0:T(8,128)S(1)}, f32[128,640]{1,0:T(8,128)S(1)}, u32[]{:S(2)}, u32[]{:S(2)}) collective-permute-start(f32[128,640]{1,0:T(8,128)S(1)} %shard_map.87), channel_id=1, source_target_pairs={{0,4},{1,5},{2,6},{3,7},{4,0},{5,1},{6,2},{7,3},{8,12},{9,13},{10,... | collective-permute-start | bytes 983048 | tf_op jit(solution)/shard_map/ppermute | solution.py:409
  (15 other events, 191.2 us)
